TPU v7x, 256 devices: a whole 4x4x8 slice. The times are simulated.
256 devices in a mesh: py: 8 (over z_lo, core), px: 32 (over y, z_hi, x).
Axes of the slice: x: 4, y: 4, z: 8 (z_hi: 2, z_lo: 4; z = z_hi * 4 + z_lo), core: 2. Of those that a mesh axis runs over, the one named last changes fastest.
Arguments:
- measured: float32 [2, 2, 8, 32, 12544], P(None, None, 'py', 'px'), may hold values from -250 to 250
- psf_taps: bfloat16 [8, 32, 32, 32, 32], P('py', 'px'), may hold values from 0 to 0.011047363
- offsets: int32 [8, 32, 2], P('py', 'px'), may hold values from 0 to 7
- window_mask: int32 [1024, 4096], P('py', 'px'), may hold values 0 or 1
Outputs:
- object_basis: float32 [2, 2, 8, 32, 12544], P(None, None, 'py', 'px')
- image_basis: float32 [2, 2, 8, 32, 12544], P(None, None, 'py', 'px')
- factors: float32 [3, 2, 2], replicated
All inputs are finite; a program needn't handle non-finite values. No bound on the sum of `window_mask` on one device may be relied on, other than what follows from the above.
Results may differ from a plain program's by a relative error of at most 0.014.
Values may be sent and summed in bfloat16 or wider, within the bound.
A program may use at most 128 MiB of HBM per device.

v0:
```python
import math

import jax
import jax.numpy as jnp
from jax import lax
from jax.sharding import PartitionSpec as P

PLANES = 2
PATCH = 128
KERNEL = 32
DEPTH_LEN = 64
HALF = 8
CORE = 112


epsilon = 1e-06


def padded_2(shard, sides, width):
    for axis, dim in sides:
        size, length = (lax.axis_size(axis), shard.shape[dim])
        up = [(i, (i + 1) % size) for i in range(size - 1)]
        down = [(j, i) for i, j in up]
        last = lax.slice_in_dim(shard, length - width, length, axis=dim)
        leading = lax.slice_in_dim(shard, 0, width, axis=dim)
        before = lax.ppermute(last, axis, up)
        after = lax.ppermute(leading, axis, down)
        shard = jnp.concatenate([before, shard, after], axis=dim)
    return shard


def twiddle(rows, cols, length, shift):
    row_ids = jnp.arange(rows, dtype=jnp.int32)[:, None]
    col_ids = jnp.arange(cols, dtype=jnp.int32)[None, :] + jnp.asarray(shift).astype(jnp.int32)
    phase = row_ids * col_ids % length
    angle = phase.astype(jnp.float32) * jnp.float32(2.0 * math.pi / length)
    return (jnp.cos(angle).astype(jnp.bfloat16), (-jnp.sin(angle)).astype(jnp.bfloat16))


def product(form, table, values):
    return jnp.einsum(form, table, values, preferred_element_type=jnp.float32)


def complex_axis(form, cos_table, sin_table, real_in, imag_in):
    real_out = product(form, cos_table, real_in) - product(form, sin_table, imag_in)
    imag_out = product(form, cos_table, imag_in) + product(form, sin_table, real_in)
    return (real_out.astype(jnp.bfloat16), imag_out.astype(jnp.bfloat16))


def spectrum(patch_taps, shift_rows, shift_cols):
    half_kernel = KERNEL // 2
    cos_x, sin_x = twiddle(PATCH, KERNEL, PATCH, shift_cols - half_kernel)
    real_x = product("fi,tji->tjf", cos_x, patch_taps).astype(jnp.bfloat16)
    imag_x = product("fi,tji->tjf", sin_x, patch_taps).astype(jnp.bfloat16)
    cos_y, sin_y = twiddle(PATCH, KERNEL, PATCH, shift_rows - half_kernel)
    real_y, imag_y = complex_axis("gj,tjf->tgf", cos_y, sin_y, real_x, imag_x)
    cos_z, sin_z = twiddle(DEPTH_LEN, KERNEL, DEPTH_LEN, -half_kernel)
    return complex_axis("qt,tgf->qgf", cos_z, sin_z, real_y, imag_y)


def blur(patch_cells, spec_real, spec_imag, adjoint):
    values = patch_cells.astype(jnp.bfloat16)
    cos_p, sin_p = twiddle(PATCH, PATCH, PATCH, 0)
    real_x = product("fx,bzyx->bzyf", cos_p, values).astype(jnp.bfloat16)
    imag_x = product("fx,bzyx->bzyf", sin_p, values).astype(jnp.bfloat16)
    real_y, imag_y = complex_axis("gy,bzyf->bzgf", cos_p, sin_p, real_x, imag_x)
    cos_z, sin_z = twiddle(DEPTH_LEN, PLANES, DEPTH_LEN, 0)
    depth_re, depth_im = complex_axis("qz,bzgf->bqgf", cos_z, sin_z, real_y, imag_y)
    kernel_re = spec_real.astype(jnp.float32)
    kernel_im = spec_imag.astype(jnp.float32)
    if adjoint:
        kernel_im = -kernel_im
    depth_re = depth_re.astype(jnp.float32)
    depth_im = depth_im.astype(jnp.float32)
    prod_re = (depth_re * kernel_re - depth_im * kernel_im).astype(jnp.bfloat16)
    prod_im = (depth_re * kernel_im + depth_im * kernel_re).astype(jnp.bfloat16)
    back_cos, back_sin = twiddle(PLANES, DEPTH_LEN, DEPTH_LEN, 0)
    plane_re, plane_im = complex_axis("zq,bqgf->bzgf", back_cos, -back_sin, prod_re, prod_im)
    row_re, row_im = complex_axis("yg,bzgf->bzyf", cos_p, -sin_p, plane_re, plane_im)
    spatial = product("xf,bzyf->bzyx", cos_p, row_re) + product("xf,bzyf->bzyx", sin_p, row_im)
    return spatial * jnp.float32(1.0 / (DEPTH_LEN * PATCH * PATCH))


def window(mask_block):
    return mask_block.astype(jnp.float32)


def fold_owned(padded, dim):
    lower = lax.slice_in_dim(padded, 0, HALF, axis=dim) + lax.slice_in_dim(
        padded, 2 * HALF, 3 * HALF, axis=dim
    )
    middle = lax.slice_in_dim(padded, 3 * HALF, PATCH - HALF, axis=dim)
    upper = lax.slice_in_dim(padded, PATCH - HALF, PATCH, axis=dim) + lax.slice_in_dim(
        padded, PATCH + HALF, PATCH + 2 * HALF, axis=dim
    )
    return jnp.concatenate([lower, middle, upper], axis=dim)


def gram_terms(pair):
    return (jnp.sum(pair[0] * pair[0]), jnp.sum(pair[0] * pair[1]), jnp.sum(pair[1] * pair[1]))


def factor(terms, count):
    r_first = jnp.sqrt(terms[0] / count + epsilon)
    r_cross = terms[1] / count / r_first
    r_second = jnp.sqrt(terms[2] / count - r_cross * r_cross + epsilon)
    return (r_first, r_cross, r_second)


def solve_right(pair, triple):
    leading = pair[0] / triple[0]
    trailing = (pair[1] - triple[1] * leading) / triple[2]
    return jnp.stack([leading, trailing])


def packed(triple):
    return jnp.stack(
        [jnp.stack([triple[0], triple[1]]), jnp.stack([jnp.zeros_like(triple[0]), triple[2]])]
    )


def flatten_cells(block):
    return block.reshape(2, PLANES, 1, 1, CORE * CORE)


def body(measured, psf_taps, offsets, window_mask):
    count_rows = lax.axis_size("py")
    count_cols = lax.axis_size("px")
    count = jnp.float32(PLANES * CORE * CORE * count_rows * count_cols)
    spec_real, spec_imag = spectrum(psf_taps[0, 0], offsets[0, 0, 0], offsets[0, 0, 1])
    weight = window(window_mask)
    first_sq, first_cross, first_tail = gram_terms(measured)
    start_terms = lax.psum((first_sq, first_cross, first_tail), ("py", "px"))
    start_factor = factor(start_terms, count)
    left_flat = solve_right(measured, start_factor)
    left_basis = left_flat.reshape(2, PLANES, CORE, CORE)
    left_narrow = left_basis.astype(jnp.bfloat16)
    left_patch = padded_2(left_narrow, (("py", 2), ("px", 3)), HALF)
    adjoint_patch = blur(left_patch, spec_real, spec_imag, True) * weight
    folded = padded_2(adjoint_patch, (("py", 2), ("px", 3)), HALF)
    adjoint_core = fold_owned(fold_owned(folded, 2), 3)
    second_sq, second_cross, second_tail = gram_terms(adjoint_core)
    alpha_terms = lax.psum((second_sq, second_cross, second_tail), ("py", "px"))
    alpha_factor = factor(alpha_terms, count)
    object_basis = solve_right(adjoint_core, alpha_factor)
    object_patch = padded_2(object_basis, (("py", 2), ("px", 3)), HALF)
    forward_patch = blur(object_patch * weight, spec_real, spec_imag, False)
    forward_padded = padded_2(forward_patch, (("py", 2), ("px", 3)), HALF)
    forward_core = fold_owned(fold_owned(forward_padded, 2), 3)
    residue = jnp.stack(
        [
            forward_core[0] - alpha_factor[0] * left_basis[0] - alpha_factor[1] * left_basis[1],
            forward_core[1] - alpha_factor[2] * left_basis[1],
        ]
    )
    third_sq, third_cross, third_tail = gram_terms(residue)
    beta_terms = lax.psum((third_sq, third_cross, third_tail), ("py", "px"))
    beta_factor = factor(beta_terms, count)
    image_basis = solve_right(residue, beta_factor)
    factors = jnp.stack([packed(start_factor), packed(alpha_factor), packed(beta_factor)])
    return (flatten_cells(object_basis), flatten_cells(image_basis), factors)


def solution(mesh):
    placed = (
        P(None, None, "py", "px", None),
        P("py", "px", None, None, None),
        P("py", "px", None),
        P("py", "px"),
    )
    return jax.shard_map(
        body,
        mesh=mesh,
        in_specs=placed,
        out_specs=(P(None, None, "py", "px", None), P(None, None, "py", "px", None), P()),
        check_vma=False,
    )
```

profile of v0, /device:TPU:1, one launch (start us, length us, event | category | flops | bytes accessed | tf_op | source)
XLA Modules:
  0.0 463.6 jit_solution(16604225201026241020)
XLA Ops:
  2.5 81.6 %all-reduce.2 = (f32[]{:T(128)}, f32[]{:T(128)}, f32[]{:T(128)}) all-reduce(f32[]{:T(128)} %get-tuple-element.14, f32[]{:T(128)} %get-tuple-element.13, f32[]{:T(128)} %get-tuple-element.12), channel_id=1, replica_groups=mesh['py'=8,'px'=32] {'py','px'}, use_global_device_ids=true, to_apply=%region_1.2 | all-reduce | flops 3 | bytes 24 | tf_op jit(solution)/shard_map/psum | solution.py:133
  88.6 2.9 collective-permute-start.1
  91.5 2.7 collective-permute-start
  100.3 1.9 copy.14
  103.8 1.9 copy.13
  107.4 4.1 fusion.387
  111.6 2.9 fusion.8
  115.9 14.7 %collective-permute-start.2 = (bf16[2,2,128,8]{3,2,1,0:T(8,128)(2,1)S(1)}, bf16[2,2,128,8]{3,2,1,0:T(8,128)(2,1)S(1)}, u32[]{:S(2)}, u32[]{:S(2)}) collective-permute-start(bf16[2,2,128,8]{3,2,1,0:T(8,128)(2,1)S(1)} %get-tuple-element.53), channel_id=1, source_target_pairs={{0,1},{1,2},{2,3},{3,4},{4,5},{5,6},{6,7},{7,8},{8,9},{9,10},{10,1... | collective-permute-start | bytes 24584 | tf_op jit(solution)/shard_map/ppermute | solution.py:26
  133.1 4.6 fusion.177
  138.2 5.4 %fusion.175 = f32[2,128,128,64]{2,3,1,0:T(8,128)} fusion(bf16[2,2,128,128]{3,1,2,0:T(2,128)(2,1)S(1)} %copy.12), kind=kOutput, calls=%fused_computation.253 | convolution fusion | flops 8390528 | bytes 8519680 | tf_op jit(solution)/shard_map/qz,bzgf->bqgf/dot_general | solution.py:41
  144.2 3.5 subtract_convert_fusion.1
  149.1 7.4 %fusion.7 = (bf16[2,64,128,128]{3,1,2,0:T(8,128)(2,1)S(1)}, bf16[2,64,128,128]{3,1,2,0:T(8,128)(2,1)S(1)}) fusion(bf16[2,128,128,64]{2,3,1,0:T(8,128)(2,1)} %subtract_convert_fusion.1, f32[64,128,128]{2,0,1:T(8,128)S(1)} %copy-done.7, f32[64,128,128]{2,0,1:T(8,128)S(1)} %copy-done.2, f32[2,128,128,64]{2,3,1,0:T(8,128)} %fusion.175, ...), kind=kOutput, calls=%fused_computation.13 | convolution fusion | flops 33556480 | bytes 29491200 | tf_op jit(solution)/shard_map/qz,bzgf->bqgf/dot_general | solution.py:41
  159.7 2.9 fusion.38
  164.3 2.2 collective-permute-start.5
  166.4 3.4 collective-permute-start.4
  172.2 4.0 collective-permute-start.6
  176.3 4.7 %collective-permute-done.7 = f32[2,2,144,8]{3,2,1,0:T(8,128)S(1)} collective-permute-done((f32[2,2,144,8]{3,2,1,0:T(8,128)S(1)}, f32[2,2,144,8]{3,2,1,0:T(8,128)S(1)}, u32[]{:S(2)}, u32[]{:S(2)}) %collective-permute-start.7) | collective-permute-done | bytes 18464 | tf_op jit(solution)/shard_map/ppermute | solution.py:27
  184.6 96.6 %all-reduce.1 = (f32[]{:T(128)}, f32[]{:T(128)}, f32[]{:T(128)}) all-reduce(f32[]{:T(128)} %get-tuple-element.11, f32[]{:T(128)} %get-tuple-element.10, f32[]{:T(128)} %get-tuple-element.9), channel_id=1, replica_groups=mesh['py'=8,'px'=32] {'py','px'}, use_global_device_ids=true, to_apply=%region_7.8 | all-reduce | flops 3 | bytes 24 | tf_op jit(solution)/shard_map/psum | solution.py:143
  284.5 3.0 collective-permute-start.9
  287.5 2.6 collective-permute-start.8
  292.5 4.2 collective-permute-start.10
  296.8 4.3 collective-permute-done.11
  304.7 4.6 fusion.173
  309.8 5.4 %fusion.171 = f32[2,128,128,64]{2,3,1,0:T(8,128)} fusion(bf16[2,2,128,128]{3,1,2,0:T(2,128)(2,1)S(1)} %copy.26), kind=kOutput, calls=%fused_computation.251 | convolution fusion | flops 8390528 | bytes 8519680 | tf_op jit(solution)/shard_map/qz,bzgf->bqgf/dot_general | solution.py:41
  315.7 3.5 subtract_convert_fusion
  320.7 7.4 %fusion.3 = (bf16[2,64,128,128]{3,1,2,0:T(8,128)(2,1)S(1)}, bf16[2,64,128,128]{3,1,2,0:T(8,128)(2,1)S(1)}) fusion(bf16[2,128,128,64]{2,3,1,0:T(8,128)(2,1)} %subtract_convert_fusion, f32[64,128,128]{2,0,1:T(8,128)S(1)} %copy-done.6, f32[64,128,128]{2,0,1:T(8,128)S(1)} %copy-done.3, f32[2,128,128,64]{2,3,1,0:T(8,128)} %fusion.171, ...), kind=kOutput, calls=%fused_computation.5 | convolution fusion | flops 33556480 | bytes 29491200 | tf_op jit(solution)/shard_map/qz,bzgf->bqgf/dot_general | solution.py:41
  331.3 2.9 fusion.31
  335.9 2.8 collective-permute-start.13
  338.6 2.8 collective-permute-start.12
  343.8 5.0 %collective-permute-start.14 = (f32[2,2,144,8]{3,2,1,0:T(8,128)S(1)}, f32[2,2,144,8]{3,2,1,0:T(8,128)S(1)}, u32[]{:S(2)}, u32[]{:S(2)}) collective-permute-start(f32[2,2,144,8]{3,2,1,0:T(8,128)S(1)} %get-tuple-element.41), channel_id=1, source_target_pairs={{0,1},{1,2},{2,3},{3,4},{4,5},{5,6},{6,7},{7,8},{8,9},{9,10},{10,1... | collective-permute-start | bytes 55304 | tf_op jit(solution)/shard_map/ppermute | solution.py:26
  349.7 4.0 collective-permute-done.15
  357.1 101.9 %all-reduce = (f32[]{:T(128)}, f32[]{:T(128)}, f32[]{:T(128)}) all-reduce(f32[]{:T(128)} %get-tuple-element.7, f32[]{:T(128)} %get-tuple-element.8, f32[]{:T(128)} %get-tuple-element.6), channel_id=1, replica_groups=mesh['py'=8,'px'=32] {'py','px'}, use_global_device_ids=true, to_apply=%region_13.14 | all-reduce | flops 3 | bytes 24 | tf_op jit(solution)/shard_map/psum | solution.py:157
  (161 shorter events, 52.8 us)
Async XLA Ops:
  0.6 95.5 %copy-start = (bf16[1,1,32,32,32]{4,3,2,1,0:T(8,128)(2,1)S(1)}, bf16[1,1,32,32,32]{4,3,2,1,0:T(8,128)(2,1)}, u32[]{:S(2)}) copy-start(bf16[1,1,32,32,32]{4,3,2,1,0:T(8,128)(2,1)} %param.5) | copy-start | bytes 196612
  88.6 10.1 %copy-start.12 = (bf16[2,2,112,112]{3,2,1,0:T(8,128)(2,1)}, bf16[2,2,112,112]{3,2,1,0:T(8,128)(2,1)S(1)}, u32[]{:S(2)}) copy-start(bf16[2,2,112,112]{3,2,1,0:T(8,128)(2,1)S(1)} %constant_dynamic-update-slice_fusion) | copy-start | bytes 301060
  88.6 25.8 %collective-permute-start.1 = (bf16[2,2,8,112]{3,2,1,0:T(8,128)(2,1)S(1)}, bf16[2,2,8,112]{3,2,1,0:T(8,128)(2,1)S(1)}, u32[]{:S(2)}, u32[]{:S(2)}) collective-permute-start(bf16[2,2,8,112]{3,2,1,0:T(8,128)(2,1)S(1)} %get-tuple-element.56), channel_id=1, source_target_pairs={{32,0},{64,32},{96,64},{128,96},{160,128},{192,160},{224,192},{33,... | collective-permute-start | bytes 21512 | tf_op jit(solution)/shard_map/ppermute | solution.py:27
  91.5 23.0 %collective-permute-start = (bf16[2,2,8,112]{3,2,1,0:T(8,128)(2,1)S(1)}, bf16[2,2,8,112]{3,2,1,0:T(8,128)(2,1)S(1)}, u32[]{:S(2)}, u32[]{:S(2)}) collective-permute-start(bf16[2,2,8,112]{3,2,1,0:T(8,128)(2,1)S(1)} %get-tuple-element.55), channel_id=1, source_target_pairs={{0,32},{32,64},{64,96},{96,128},{128,160},{160,192},{192,224},{1,3... | collective-permute-start | bytes 21512 | tf_op jit(solution)/shard_map/ppermute | solution.py:26
  96.5 1.1 copy-start.10
  98.1 4.1 copy-start.11
  111.6 2.9 copy-start.13
  111.6 19.0 %copy-start.15 = (s32[128,128]{1,0:T(8,128)S(1)}, s32[128,128]{1,0:T(8,128)}, u32[]{:S(2)}) copy-start(s32[128,128]{1,0:T(8,128)} %param.7) | copy-start | bytes 196612
  114.6 16.0 %collective-permute-start.3 = (bf16[2,2,128,8]{3,2,1,0:T(8,128)(2,1)S(1)}, bf16[2,2,128,8]{3,2,1,0:T(8,128)(2,1)S(1)}, u32[]{:S(2)}, u32[]{:S(2)}) collective-permute-start(bf16[2,2,128,8]{3,2,1,0:T(8,128)(2,1)S(1)} %get-tuple-element.54), channel_id=1, source_target_pairs={{1,0},{2,1},{3,2},{4,3},{5,4},{6,5},{7,6},{8,7},{9,8},{10,9},{11,1... | collective-permute-start | bytes 24584 | tf_op jit(solution)/shard_map/ppermute | solution.py:27
  115.9 14.7 %collective-permute-start.2 = (bf16[2,2,128,8]{3,2,1,0:T(8,128)(2,1)S(1)}, bf16[2,2,128,8]{3,2,1,0:T(8,128)(2,1)S(1)}, u32[]{:S(2)}, u32[]{:S(2)}) collective-permute-start(bf16[2,2,128,8]{3,2,1,0:T(8,128)(2,1)S(1)} %get-tuple-element.53), channel_id=1, source_target_pairs={{0,1},{1,2},{2,3},{3,4},{4,5},{5,6},{6,7},{7,8},{8,9},{9,10},{10,1... | collective-permute-start | bytes 24584 | tf_op jit(solution)/shard_map/ppermute | solution.py:26
  138.2 5.9 %copy-start.8 = (f32[2,128,128,64]{2,3,1,0:T(8,128)S(1)}, f32[2,128,128,64]{2,3,1,0:T(8,128)}, u32[]{:S(2)}) copy-start(f32[2,128,128,64]{2,3,1,0:T(8,128)} %fusion.177) | copy-start | bytes 25165828
  144.1 3.5 copy-start.2
  144.2 5.0 %copy-start.7 = (f32[64,128,128]{2,0,1:T(8,128)S(1)}, f32[64,128,128]{2,0,1:T(8,128)}, u32[]{:S(2)}) copy-start(f32[64,128,128]{2,0,1:T(8,128)} %get-tuple-element.59) | copy-start | bytes 12582916
  156.5 1.9 copy-start.5
  164.3 5.6 %collective-permute-start.5 = (f32[2,2,8,128]{3,2,1,0:T(8,128)S(1)}, f32[2,2,8,128]{3,2,1,0:T(8,128)S(1)}, u32[]{:S(2)}, u32[]{:S(2)}) collective-permute-start(f32[2,2,8,128]{3,2,1,0:T(8,128)S(1)} %get-tuple-element.50), channel_id=1, source_target_pairs={{32,0},{64,32},{96,64},{128,96},{160,128},{192,160},{224,192},{33,... | collective-permute-start | bytes 49160 | tf_op jit(solution)/shard_map/ppermute | solution.py:27
  166.4 4.3 collective-permute-start.4
  170.9 10.1 %collective-permute-start.7 = (f32[2,2,144,8]{3,2,1,0:T(8,128)S(1)}, f32[2,2,144,8]{3,2,1,0:T(8,128)S(1)}, u32[]{:S(2)}, u32[]{:S(2)}) collective-permute-start(f32[2,2,144,8]{3,2,1,0:T(8,128)S(1)} %get-tuple-element.44), channel_id=1, source_target_pairs={{1,0},{2,1},{3,2},{4,3},{5,4},{6,5},{7,6},{8,7},{9,8},{10,9},{11,1... | collective-permute-start | bytes 55304 | tf_op jit(solution)/shard_map/ppermute | solution.py:27
  172.2 10.5 %collective-permute-start.6 = (f32[2,2,144,8]{3,2,1,0:T(8,128)S(1)}, f32[2,2,144,8]{3,2,1,0:T(8,128)S(1)}, u32[]{:S(2)}, u32[]{:S(2)}) collective-permute-start(f32[2,2,144,8]{3,2,1,0:T(8,128)S(1)} %get-tuple-element.43), channel_id=1, source_target_pairs={{0,1},{1,2},{2,3},{3,4},{4,5},{5,6},{6,7},{7,8},{8,9},{9,10},{10,1... | collective-permute-start | bytes 55304 | tf_op jit(solution)/shard_map/ppermute | solution.py:26
  183.0 100.6 %copy-start.14 = (f32[1,2,1,1,12544]{4,3,2,1,0:T(1,128)S(1)}, f32[1,2,1,1,12544]{4,3,2,1,0:T(1,128)}, u32[]{:S(2)}) copy-start(f32[1,2,1,1,12544]{4,3,2,1,0:T(1,128)} %get-tuple-element.31) | copy-start | bytes 301060
  284.5 6.5 %collective-permute-start.9 = (f32[2,2,8,112]{3,2,1,0:T(8,128)S(1)}, f32[2,2,8,112]{3,2,1,0:T(8,128)S(1)}, u32[]{:S(2)}, u32[]{:S(2)}) collective-permute-start(f32[2,2,8,112]{3,2,1,0:T(8,128)S(1)} %get-tuple-element.52), channel_id=1, source_target_pairs={{32,0},{64,32},{96,64},{128,96},{160,128},{192,160},{224,192},{33,... | collective-permute-start | bytes 43016 | tf_op jit(solution)/shard_map/ppermute | solution.py:27
  287.5 3.5 collective-permute-start.8
  291.2 9.9 %collective-permute-start.11 = (f32[2,2,128,8]{3,2,1,0:T(8,128)S(1)}, f32[2,2,128,8]{3,2,1,0:T(8,128)S(1)}, u32[]{:S(2)}, u32[]{:S(2)}) collective-permute-start(f32[2,2,128,8]{3,2,1,0:T(8,128)S(1)} %get-tuple-element.48), channel_id=1, source_target_pairs={{1,0},{2,1},{3,2},{4,3},{5,4},{6,5},{7,6},{8,7},{9,8},{10,9},{11,1... | collective-permute-start | bytes 49160 | tf_op jit(solution)/shard_map/ppermute | solution.py:27
  292.5 9.7 %collective-permute-start.10 = (f32[2,2,128,8]{3,2,1,0:T(8,128)S(1)}, f32[2,2,128,8]{3,2,1,0:T(8,128)S(1)}, u32[]{:S(2)}, u32[]{:S(2)}) collective-permute-start(f32[2,2,128,8]{3,2,1,0:T(8,128)S(1)} %get-tuple-element.47), channel_id=1, source_target_pairs={{0,1},{1,2},{2,3},{3,4},{4,5},{5,6},{6,7},{7,8},{8,9},{9,10},{10,1... | collective-permute-start | bytes 49160 | tf_op jit(solution)/shard_map/ppermute | solution.py:26
  309.8 5.9 %copy-start.9 = (f32[2,128,128,64]{2,3,1,0:T(8,128)S(1)}, f32[2,128,128,64]{2,3,1,0:T(8,128)}, u32[]{:S(2)}) copy-start(f32[2,128,128,64]{2,3,1,0:T(8,128)} %fusion.173) | copy-start | bytes 25165828
  315.7 3.5 copy-start.3
  315.7 5.0 %copy-start.6 = (f32[64,128,128]{2,0,1:T(8,128)S(1)}, f32[64,128,128]{2,0,1:T(8,128)}, u32[]{:S(2)}) copy-start(f32[64,128,128]{2,0,1:T(8,128)} %get-tuple-element.60) | copy-start | bytes 12582916
  328.1 1.9 copy-start.4
  335.9 5.6 %collective-permute-start.13 = (f32[2,2,8,128]{3,2,1,0:T(8,128)S(1)}, f32[2,2,8,128]{3,2,1,0:T(8,128)S(1)}, u32[]{:S(2)}, u32[]{:S(2)}) collective-permute-start(f32[2,2,8,128]{3,2,1,0:T(8,128)S(1)} %get-tuple-element.46), channel_id=1, source_target_pairs={{32,0},{64,32},{96,64},{128,96},{160,128},{192,160},{224,192},{33,... | collective-permute-start | bytes 49160 | tf_op jit(solution)/shard_map/ppermute | solution.py:27
  338.6 3.6 collective-permute-start.12
  342.5 11.2 %collective-permute-start.15 = (f32[2,2,144,8]{3,2,1,0:T(8,128)S(1)}, f32[2,2,144,8]{3,2,1,0:T(8,128)S(1)}, u32[]{:S(2)}, u32[]{:S(2)}) collective-permute-start(f32[2,2,144,8]{3,2,1,0:T(8,128)S(1)} %get-tuple-element.42), channel_id=1, source_target_pairs={{1,0},{2,1},{3,2},{4,3},{5,4},{6,5},{7,6},{8,7},{9,8},{10,9},{11,1... | collective-permute-start | bytes 55304 | tf_op jit(solution)/shard_map/ppermute | solution.py:27
  343.8 11.5 %collective-permute-start.14 = (f32[2,2,144,8]{3,2,1,0:T(8,128)S(1)}, f32[2,2,144,8]{3,2,1,0:T(8,128)S(1)}, u32[]{:S(2)}, u32[]{:S(2)}) collective-permute-start(f32[2,2,144,8]{3,2,1,0:T(8,128)S(1)} %get-tuple-element.41), channel_id=1, source_target_pairs={{0,1},{1,2},{2,3},{3,4},{4,5},{5,6},{6,7},{7,8},{8,9},{9,10},{10,1... | collective-permute-start | bytes 55304 | tf_op jit(solution)/shard_map/ppermute | solution.py:26
  355.2 107.9 %copy-start.1 = (bf16[1,1,32,32,32]{4,3,2,1,0:T(8,128)(2,1)S(1)}, bf16[1,1,32,32,32]{4,3,2,1,0:T(8,128)(2,1)}, u32[]{:S(2)}) copy-start(bf16[1,1,32,32,32]{4,3,2,1,0:T(8,128)(2,1)} %param.5) | copy-start | bytes 196612
where the time goes:
time: 468 us; the launch traced here: 464 us
  blocking collectives  280 us (60%)
  matrix products  74.1 us (16%)
  starting transfers between devices  55.3 us (12%)
  waiting for transfers between devices  19 us (4%)
  local copies, waits for them, and re-layouts  14.9 us (3%)
  other arithmetic  10.9 us (2%)
  between operations  9.35 us (2%)
    psum x1, blocking collectives, body(): beta_terms = lax.psum((third_sq, third_cross, third_tail), ('py', 'px'))  102 us
    psum x1, blocking collectives, body(): alpha_terms = lax.psum((second_sq, second_cross, second_tail), ('py', 'px'))  96.6 us
    psum x1, blocking collectives, body(): start_terms = lax.psum((first_sq, first_cross, first_tail), ('py', 'px'))  81.6 us
    dot_general x46, matrix products, product(): return jnp.einsum(form, table, values, preferred_element_type=jnp.float32)  74.1 us
    ppermute x8, starting transfers between devices, padded_2(): before = lax.ppermute(last, axis, up)  39.4 us
    ppermute x8, starting transfers between devices, padded_2(): after = lax.ppermute(leading, axis, down)  15.9 us
    ppermute x8, waiting for transfers between devices, padded_2(): after = lax.ppermute(leading, axis, down)  13.1 us
  transfers between devices with their start and end apart: 16, of which 8 were waited for; matrix products, arithmetic and copies ran while one was open for 4% of the time, Pallas kernels for 0%

commit v1 on v0

v1 whole, which is shorter than its diff:
```python
import functools
import math

import jax
import jax.numpy as jnp
import numpy as np
from jax import lax
from jax.experimental import pallas as pl
from jax.experimental.pallas import tpu as pltpu
from jax.sharding import PartitionSpec as P

PLANES = 2
PATCH = 128
KERNEL = 32
HALF = 8
CORE = 112
FLAT = 2 * PLANES * CORE * CORE // 128
TAP = KERNEL // 2 - 1
EPSILON = 1e-06
F32 = jnp.float32
BF16 = jnp.bfloat16


def tables():
    ids = np.arange(PATCH)
    angle = 2 * np.pi * (np.outer(ids, ids) % PATCH) / PATCH
    cos, sin = np.cos(angle), -np.sin(angle)
    forward = np.block([[cos, sin], [-sin, cos]])
    places = np.arange(64) - KERNEL // 2
    angle = 2 * np.pi * (np.outer(places, ids) % PATCH) / PATCH
    cos, sin = np.cos(angle), -np.sin(angle)
    taps_x = np.concatenate([cos, sin], axis=1)
    taps_y = np.block([[cos.T, -sin.T], [sin.T, cos.T]])
    return [jnp.asarray(t, BF16) for t in (forward, forward.T, taps_x, taps_y)]


def mm(left, right):
    return jnp.dot(left, right, preferred_element_type=F32)


def roll(values, shift):
    shift = shift % 128
    return values if shift == 0 else pltpu.roll(values, shift, 1)


def total(values):
    return jnp.sum(jnp.sum(values, axis=0, keepdims=True), axis=1, keepdims=True)


class Exchange:
    def __init__(self, index, ny, nx, height, rows, cols, planes, packed, turned, row_in, col_in, corner_in, send, recv):
        self.index, self.height = index, height
        self.planes, self.packed, self.turned = planes, packed, turned
        self.row_in, self.col_in, self.corner_in = row_in, col_in, corner_in
        py, px = lax.axis_index("py"), lax.axis_index("px")
        up, down = lax.rem(py + ny - 1, ny), lax.rem(py + 1, ny)
        left, right = lax.rem(px + nx - 1, nx), lax.rem(px + 1, nx)
        top, bottom = pl.ds(rows[0], height), pl.ds(rows[1], height)
        (left_from, left_to), (right_from, right_to) = cols
        plan = [
            (planes.at[:, top, :], row_in.at[1], up, px),
            (planes.at[:, bottom, :], row_in.at[0], down, px),
            (turned.at[:, pl.ds(left_from, height), :], col_in.at[:, pl.ds(left_to, height), :], py, left),
            (turned.at[:, pl.ds(right_from, height), :], col_in.at[:, pl.ds(right_to, height), :], py, right),
            (packed.at[top, :], corner_in.at[3], up, left),
            (packed.at[top, :], corner_in.at[2], up, right),
            (packed.at[bottom, :], corner_in.at[1], down, left),
            (packed.at[bottom, :], corner_in.at[0], down, right),
        ]
        self.copies = [
            pltpu.make_async_remote_copy(
                src_ref=source,
                dst_ref=target,
                send_sem=send.at[index, i],
                recv_sem=recv.at[index, i],
                device_id={"py": to_y, "px": to_x},
                device_id_type=pl.DeviceIdType.MESH,
            )
            for i, (source, target, to_y, to_x) in enumerate(plan)
        ]

    def start(self):
        lane = lax.broadcasted_iota(jnp.int32, (PATCH, 128), 1)
        for copy in self.copies[:2]:
            copy.start()
        packed = roll(self.planes[0], 16)
        for m in range(1, 2 * PLANES):
            packed = jnp.where(lane >= 32 * m, roll(self.planes[m], 16 + 32 * m), packed)
        self.packed[...] = packed
        self.turned[...] = packed.T.reshape(2 * PLANES, 32, PATCH)
        for copy in self.copies[2:]:
            copy.start()

    def wait_recv(self):
        for copy in self.copies:
            copy.wait_recv()

    def wait_send(self):
        for copy in self.copies:
            copy.wait_send()

    def sides(self):
        columns = self.col_in[...].reshape(4 * 32, PATCH).T
        lane = lax.broadcasted_iota(jnp.int32, (self.height, 128), 1)
        is_left = lax.rem(lane, 32) >= 16
        upper = jnp.where(is_left, roll(self.corner_in[0], 16), roll(self.corner_in[1], -16))
        lower = jnp.where(is_left, roll(self.corner_in[2], 16), roll(self.corner_in[3], -16))
        return columns, upper, lower


def normalised(cells):
    s00 = sum(total(cells[0][z] * cells[0][z]) for z in range(PLANES))
    s01 = sum(total(cells[0][z] * cells[1][z]) for z in range(PLANES))
    s11 = sum(total(cells[1][z] * cells[1][z]) for z in range(PLANES))
    tiny = F32(1e-30)
    q0 = lax.rsqrt(jnp.maximum(s00, tiny))
    cross = s01 * q0
    q1 = lax.rsqrt(jnp.maximum(s11 - cross * cross, s11 * F32(1e-6) + tiny))
    first = [cells[0][z] * q0 for z in range(PLANES)]
    second = [(cells[1][z] - cross * first[z]) * q1 for z in range(PLANES)]
    return (first, second), (1.0 / q0, cross, 1.0 / q1)


def blur(cells, spectrum, forward_ref, backward_ref, adjoint):
    half = PATCH
    table, turned = forward_ref[...], backward_ref[...]
    values = jnp.concatenate(
        [jnp.concatenate([cells[k][z].astype(BF16) for k in range(2)], axis=1) for z in range(PLANES)], axis=0
    )
    along_x = mm(values, table).astype(BF16)
    swapped = jnp.concatenate(
        [
            jnp.concatenate([along_x[z * half : (z + 1) * half, c * half : (c + 1) * half] for z in range(PLANES)], axis=1)
            for c in range(2)
        ],
        axis=0,
    )
    along_y = mm(turned, swapped)
    re = [along_y[:half, z * half : (z + 1) * half] for z in range(PLANES)]
    im = [along_y[half:, z * half : (z + 1) * half] for z in range(PLANES)]
    tap_re = [spectrum[:half, t * half : (t + 1) * half] for t in range(3)]
    tap_im = [spectrum[half:, t * half : (t + 1) * half] for t in range(3)]
    sign = -1.0 if adjoint else 1.0
    out_re, out_im = [], []
    for z_out in range(PLANES):
        sum_re = sum_im = None
        for z_in in range(PLANES):
            depth = 1 + (z_in - z_out) if adjoint else 1 - (z_in - z_out)
            a, b = tap_re[depth], sign * tap_im[depth]
            part_re = re[z_in] * a - im[z_in] * b
            part_im = re[z_in] * b + im[z_in] * a
            sum_re = part_re if sum_re is None else sum_re + part_re
            sum_im = part_im if sum_im is None else sum_im + part_im
        out_re.append(sum_re.astype(BF16))
        out_im.append(sum_im.astype(BF16))
    product = jnp.concatenate([jnp.concatenate(out_re, axis=1), jnp.concatenate(out_im, axis=1)], axis=0)
    back_y = mm(table, product).astype(BF16)
    swapped = jnp.concatenate(
        [
            jnp.concatenate([back_y[c * half : (c + 1) * half, z * half : (z + 1) * half] for c in range(2)], axis=1)
            for z in range(PLANES)
        ],
        axis=0,
    )
    back_x = mm(swapped, turned)
    return [[back_x[z * half : (z + 1) * half, k * half : (k + 1) * half] for z in range(PLANES)] for k in range(2)]


def restored(cells, factor):
    first = [factor[0] * cells[0][z] for z in range(PLANES)]
    second = [factor[2] * cells[1][z] + factor[1] * cells[0][z] for z in range(PLANES)]
    return first, second


def factor_of(g00, g01, g11):
    r00 = jnp.sqrt(jnp.maximum(g00, 0.0) + EPSILON)
    r01 = g01 / r00
    r11 = jnp.sqrt(jnp.maximum(g11 - r01 * r01, 0.0) + EPSILON)
    return r00, r01, r11


def kernel(
    ny, nx,
    measured_hbm, taps_hbm, offsets, mask_hbm, forward_hbm, backward_hbm, taps_x_hbm, taps_y_hbm,
    object_hbm, image_hbm, factors_ref,
    measured, taps, mask, forward_ref, backward_ref, taps_x, taps_y,
    spectrum_ref, planes, packed, turned, row8, col_in, corner8, row16, corner16,
    object_flat, forward_flat, image_flat, grid_ref,
    one_out, one_in, two_out, two_in,
    load_sem, store_sem, send_sem, recv_sem, sum_send, sum_recv,
):
    py, px = lax.axis_index("py"), lax.axis_index("px")
    loads = [
        pltpu.make_async_copy(source, target, load_sem.at[i])
        for i, (source, target) in enumerate(
            [
                (measured_hbm, measured),
                (taps_hbm.at[0, 0, pl.ds(TAP, 3)], taps),
                (taps_x_hbm, taps_x),
                (taps_y_hbm, taps_y),
                (mask_hbm, mask),
                (forward_hbm, forward_ref),
                (backward_hbm, backward_ref),
            ]
        )
    ]
    for load in loads:
        load.start()

    row, high, column = px // 8, lax.rem(px // 4, 2), lax.rem(px, 4)
    place_one, place_two = high * ny + py, row * 4 + column

    def partner_one(step):
        at = lax.rem(place_one + step, 16)
        return {"py": lax.rem(at, ny), "px": row * 8 + (at // ny) * 4 + column}

    def partner_two(step):
        at = lax.rem(place_two + step, 16)
        return {"py": py, "px": (at // 4) * 8 + high * 4 + lax.rem(at, 4)}

    exchange = functools.partial(Exchange, ny=ny, nx=nx, send=send_sem, recv=recv_sem)
    first = exchange(
        index=0, height=8, rows=(8, 112), cols=((24, 8), (0, 16)), planes=planes.at[0], packed=packed.at[0],
        turned=turned.at[0], row_in=row8.at[0], col_in=col_in.at[0], corner_in=corner8.at[0],
    )
    second = exchange(
        index=1, height=16, rows=(0, 112), cols=((16, 0), (0, 16)), planes=planes.at[1], packed=packed.at[1],
        turned=turned.at[1], row_in=row16, col_in=col_in.at[1], corner_in=corner16,
    )
    third = exchange(
        index=2, height=8, rows=(0, 120), cols=((16, 0), (8, 24)), planes=planes.at[2], packed=packed.at[2],
        turned=turned.at[2], row_in=row8.at[1], col_in=col_in.at[2], corner_in=corner8.at[1],
    )
    barrier = pltpu.get_barrier_semaphore()
    greeted = 0
    for dy in (ny - 1, 0, 1):
        for dx in (nx - 1, 0, 1):
            if dy or dx:
                to = {"py": lax.rem(py + dy, ny), "px": lax.rem(px + dx, nx)}
                pl.semaphore_signal(barrier, inc=1, device_id=to, device_id_type=pl.DeviceIdType.MESH)
                greeted += 1
    for step in range(1, 16):
        for to in (partner_one(step), partner_two(step)):
            pl.semaphore_signal(barrier, inc=1, device_id=to, device_id_type=pl.DeviceIdType.MESH)
            greeted += 1

    lane = lax.broadcasted_iota(jnp.int32, (PATCH, 128), 1)
    line = lax.broadcasted_iota(jnp.int32, (PATCH, 128), 0)
    owned_lane = (lane >= HALF) & (lane < PATCH - HALF)
    has_up, has_down, has_left, has_right = py > 0, py < ny - 1, px > 0, px < nx - 1
    low_y, high_y = jnp.where(has_up, 0, HALF), jnp.where(has_down, PATCH, PATCH - HALF)
    low_x, high_x = jnp.where(has_left, 0, HALF), jnp.where(has_right, PATCH, PATCH - HALF)
    inside = (line >= low_y) & (line < high_y) & (lane >= low_x) & (lane < high_x)

    loads[0].wait()
    lane14 = lax.broadcasted_iota(jnp.int32, (14, 128), 1)
    for m in range(4):
        planes[0, m, 0:HALF, :] = jnp.zeros((HALF, 128), F32)
        planes[0, m, PATCH - HALF : PATCH, :] = jnp.zeros((HALF, 128), F32)
        for k in range(8):
            if k < 7:
                high_part = measured[pl.ds(98 * m + k, 14, stride=7), :]
            if k == 0:
                both = high_part
            elif k == 7:
                both = measured[pl.ds(98 * m + 6, 14, stride=7), :]
            else:
                low_part = measured[pl.ds(98 * m + k - 1, 14, stride=7), :]
                both = jnp.where(lane14 >= 128 - 16 * k, low_part, high_part)
            planes[0, m, pl.ds(HALF + k, 14, stride=8), :] = roll(both, 16 * k + HALF)

    pl.semaphore_wait(barrier, greeted)
    first.start()

    for load in loads[1:4]:
        load.wait()
    shift_y, shift_x = offsets[0, 0, 0], offsets[0, 0, 1]
    pick_x = (
        lax.broadcasted_iota(jnp.int32, (KERNEL, 64), 1) == lax.broadcasted_iota(jnp.int32, (KERNEL, 64), 0) + shift_x
    )
    pick_y = (
        lax.broadcasted_iota(jnp.int32, (64, KERNEL), 0) == lax.broadcasted_iota(jnp.int32, (64, KERNEL), 1) + shift_y
    )
    pick_x = jnp.where(pick_x, 1.0, 0.0).astype(BF16)
    pick_y = jnp.where(pick_y, 1.0, 0.0).astype(BF16)
    placed = mm(taps[...].reshape(3 * KERNEL, KERNEL), pick_x).astype(BF16)
    kx = mm(placed, taps_x[...]).astype(BF16)
    side_by_side = jnp.concatenate([kx[t * KERNEL : (t + 1) * KERNEL] for t in range(3)], axis=1)
    kx = mm(pick_y, side_by_side).astype(BF16)
    kx = jnp.concatenate(
        [
            jnp.concatenate([kx[:, t * 256 + c * 128 : t * 256 + (c + 1) * 128] for t in range(3)], axis=1)
            for c in range(2)
        ],
        axis=0,
    )
    spectrum_ref[...] = mm(taps_y[...], kx) * F32(1.0 / (PATCH * PATCH))

    for load in loads[4:]:
        load.wait()
    weight = mask[...].astype(F32)

    def tile(left, right):
        return jnp.sum((left * right).reshape(-1, 8, 128), axis=0)

    owned = slice(HALF, PATCH - HALF)
    owned_core = owned_lane[owned]
    own_m = [[jnp.where(owned_core, planes[0, 2 * k + z, owned, :], 0.0) for z in range(PLANES)] for k in range(2)]

    def grams(left, right, pairs):
        return [sum(tile(left[i][z], right[j][z]) for z in range(PLANES)) for i, j in pairs]

    sums = grams(own_m, own_m, ((0, 0), (0, 1), (1, 1)))

    first.wait_recv()
    columns, upper, lower = first.sides()
    columns = jnp.concatenate([upper, columns[owned], lower], axis=0)
    window = [[None, None], [None, None]]
    for m in range(4):
        centre = jnp.concatenate([row8[0, 0, m], planes[0, m, owned, :], row8[0, 1, m]], axis=0)
        cells = jnp.where(owned_lane, centre, roll(columns, -16 - 32 * m))
        window[m // 2][m % 2] = jnp.where(inside, cells, 0.0)
    unit, factor = normalised(window)
    result = restored(blur(unit, spectrum_ref[...], forward_ref, backward_ref, True), factor)
    for m in range(4):
        planes[1, m] = result[m // 2][m % 2] * weight
    second.start()
    first.wait_send()

    second.wait_recv()
    columns, upper, lower = second.sides()
    upper, lower = jnp.where(has_up, upper, 0.0), jnp.where(has_down, lower, 0.0)
    columns = jnp.concatenate([columns[:16] + upper, columns[16:112], columns[112:] + lower], axis=0)
    edge_lane = ((lane < 16) & has_left) | ((lane >= 112) & has_right)
    second.wait_send()
    window = [[None, None], [None, None]]
    own_v = [[None, None], [None, None]]
    keep = jnp.where(inside, weight, 0.0)
    for m in range(4):
        cells = planes[1, m]
        up_rows = jnp.where(has_up, row16[0, m], 0.0)
        down_rows = jnp.where(has_down, row16[1, m], 0.0)
        cells = jnp.concatenate([cells[:16] + up_rows, cells[16:112], cells[112:] + down_rows], axis=0)
        cells = cells + jnp.where(edge_lane, roll(columns, -16 - 32 * m), 0.0)
        planes[1, m] = cells
        own_v[m // 2][m % 2] = jnp.where(owned_core, cells[owned], 0.0)
        window[m // 2][m % 2] = cells * keep
    sums += grams(own_v, own_v, ((0, 0), (0, 1), (1, 1)))
    unit, factor = normalised(window)
    result = restored(blur(unit, spectrum_ref[...], forward_ref, backward_ref, False), factor)
    for m in range(4):
        planes[2, m] = result[m // 2][m % 2]
    third.start()

    def to_flat(source, target):
        for m in range(4):
            for j in range(7):
                head = roll(source(m, pl.ds(HALF + j, 14, stride=8)), -16 * j - HALF)
                tail = roll(source(m, pl.ds(HALF + j + 1, 14, stride=8)), 104 - 16 * j)
                target[pl.ds(98 * m + j, 14, stride=7), :] = jnp.where(lane14 < 112 - 16 * j, head, tail)

    to_flat(lambda m, rows: planes[1, m, rows, :], object_flat)

    third.wait_recv()
    columns, upper, lower = third.sides()
    upper, lower = jnp.where(has_up, upper, 0.0), jnp.where(has_down, lower, 0.0)
    columns = jnp.concatenate([columns[:8], columns[8:16] + upper, columns[16:112], columns[112:120] + lower, columns[120:]], axis=0)
    third.wait_send()
    edge_lane = ((lane >= 8) & (lane < 16) & has_left) | ((lane >= 112) & (lane < 120) & has_right)
    own_f = [[None, None], [None, None]]
    for m in range(4):
        cells = planes[2, m]
        up_rows = jnp.where(has_up, row8[1, 0, m], 0.0)
        down_rows = jnp.where(has_down, row8[1, 1, m], 0.0)
        cells = jnp.concatenate([cells[8:16] + up_rows, cells[16:112], cells[112:120] + down_rows], axis=0)
        cells = cells + jnp.where(edge_lane[owned], roll(columns[owned], -16 - 32 * m), 0.0)
        cells = jnp.where(owned_core, cells, 0.0)
        planes[2, m, owned, :] = cells
        own_f[m // 2][m % 2] = cells
    sums += grams(own_f, own_f, ((0, 0), (0, 1), (1, 1)))
    sums += grams(own_f, own_m, ((0, 0), (0, 1), (1, 0), (1, 1)))

    line16 = lax.broadcasted_iota(jnp.int32, (16, 128), 0)
    lane16 = lax.broadcasted_iota(jnp.int32, (16, 128), 1)
    stacked = jnp.zeros((16, 128), F32)
    for q, values in enumerate(sums):
        stacked = jnp.where(line16 == q, jnp.sum(values, axis=0, keepdims=True), stacked)
    stacked = jnp.sum(stacked, axis=1, keepdims=True)
    mine = jnp.sum(jnp.where(line16 == lane16, stacked, 0.0), axis=0, keepdims=True)

    def all_sum(mine, out_ref, in_ref, place, partner, stage):
        out_ref[...] = mine
        in_ref[place] = mine
        copies = [
            pltpu.make_async_remote_copy(
                src_ref=out_ref,
                dst_ref=in_ref.at[place],
                send_sem=sum_send.at[stage, step],
                recv_sem=sum_recv.at[stage, step],
                device_id=partner(step),
                device_id_type=pl.DeviceIdType.MESH,
            )
            for step in range(1, 16)
        ]
        for copy in copies:
            copy.start()
        return copies

    copies = all_sum(mine, one_out, one_in, place_one, partner_one, 0)
    to_flat(lambda m, rows: planes[2, m, rows, :], forward_flat)
    for copy in copies:
        copy.wait()
    mine = jnp.sum(one_in[...], axis=0)
    copies = all_sum(mine, two_out, two_in, place_two, partner_two, 1)
    for copy in copies:
        copy.wait()
    cells_total = PLANES * CORE * CORE * ny * nx
    gathered = jnp.sum(two_in[...], axis=0) * F32(1.0 / cells_total)
    lane1 = lax.broadcasted_iota(jnp.int32, (1, 128), 1)
    m00, m01, m11, v00, v01, v11, f00, f01, f11, p00, p01, p10, p11 = [
        jnp.sum(jnp.where(lane1 == q, gathered, 0.0), axis=1, keepdims=True) for q in range(13)
    ]
    a, b, c = factor_of(m00, m01, m11)
    u00, u11 = 1.0 / a, 1.0 / c
    u01 = -b * u00 * u11
    w00 = u00 * u00 * v00
    w01 = u00 * (u01 * v00 + u11 * v01)
    w11 = u01 * u01 * v00 + 2.0 * u01 * u11 * v01 + u11 * u11 * v11
    alpha, beta, gamma = factor_of(w00, w01, w11)
    t00 = u00 / alpha
    t11 = u11 / gamma
    t01 = (u01 - beta * t00) / gamma
    x0, x1 = alpha * u00 + beta * u01, beta * u11
    y0, y1 = gamma * u01, gamma * u11

    def form(l, r):
        return (
            l[0] * (r[0] * f00 + r[1] * f01 - r[2] * p00 - r[3] * p01)
            + l[1] * (r[0] * f01 + r[1] * f11 - r[2] * p10 - r[3] * p11)
            - l[2] * (r[0] * p00 + r[1] * p10 - r[2] * m00 - r[3] * m01)
            - l[3] * (r[0] * p01 + r[1] * p11 - r[2] * m01 - r[3] * m11)
        )

    zero = jnp.zeros_like(a)
    z_first, z_second = (t00, zero, x0, x1), (t01, t11, y0, y1)
    rho, sigma, tau = factor_of(form(z_first, z_first), form(z_first, z_second), form(z_second, z_second))
    i0 = [value / rho for value in z_first]
    i1 = [(value - sigma * lead) / tau for value, lead in zip(z_second, i0)]

    half = FLAT // 2
    one, two = slice(0, half), slice(half, FLAT)
    v_one, v_two = object_flat[one, :], object_flat[two, :]
    f_one, f_two = forward_flat[one, :], forward_flat[two, :]
    m_one, m_two = measured[one, :], measured[two, :]
    object_flat[one, :] = t00 * v_one
    object_flat[two, :] = t01 * v_one + t11 * v_two
    image_flat[one, :] = i0[0] * f_one - i0[2] * m_one - i0[3] * m_two
    image_flat[two, :] = i1[0] * f_one + i1[1] * f_two - i1[2] * m_one - i1[3] * m_two
    stores = [
        pltpu.make_async_copy(object_flat, object_hbm, store_sem.at[0]),
        pltpu.make_async_copy(image_flat, image_hbm, store_sem.at[1]),
    ]
    for store in stores:
        store.start()
    which = lax.broadcasted_iota(jnp.int32, (3, 2, 2), 0)
    down = lax.broadcasted_iota(jnp.int32, (3, 2, 2), 1)
    across = lax.broadcasted_iota(jnp.int32, (3, 2, 2), 2)
    factors = jnp.zeros((3, 2, 2), F32)
    for i, triple in enumerate(((a, b, c), (alpha, beta, gamma), (rho, sigma, tau))):
        for (r, k), value in zip(((0, 0), (0, 1), (1, 1)), triple):
            here = (which == i) & (down == r) & (across == k)
            factors = jnp.where(here, value.reshape(1, 1, 1), factors)
    factors_ref[...] = factors
    for store in stores:
        store.wait()


def body(measured, psf_taps, offsets, window_mask):
    ny, nx = lax.axis_size("py"), lax.axis_size("px")
    any_space = pl.BlockSpec(memory_space=pl.ANY)
    vmem = pl.BlockSpec(memory_space=pltpu.VMEM)
    smem = pl.BlockSpec(memory_space=pltpu.SMEM)
    flat = jax.ShapeDtypeStruct((FLAT, 128), F32)
    forward, backward, taps_x, taps_y = tables()
    objects, images, factors = pl.pallas_call(
        functools.partial(kernel, ny, nx),
        out_shape=(flat, flat, jax.ShapeDtypeStruct((3, 2, 2), F32)),
        in_specs=[any_space, any_space, smem, any_space, any_space, any_space, any_space, any_space],
        out_specs=(any_space, any_space, vmem),
        scratch_shapes=[
            pltpu.VMEM((FLAT, 128), F32),
            pltpu.VMEM((3, KERNEL, KERNEL), BF16),
            pltpu.VMEM((PATCH, PATCH), jnp.int32),
            pltpu.VMEM((256, 256), BF16),
            pltpu.VMEM((256, 256), BF16),
            pltpu.VMEM((64, 256), BF16),
            pltpu.VMEM((256, 128), BF16),
            pltpu.VMEM((256, 384), F32),
            pltpu.VMEM((3, 4, PATCH, 128), F32),
            pltpu.VMEM((3, PATCH, 128), F32),
            pltpu.VMEM((3, 4, 32, PATCH), F32),
            pltpu.VMEM((2, 2, 4, 8, 128), F32),
            pltpu.VMEM((3, 4, 32, PATCH), F32),
            pltpu.VMEM((2, 4, 8, 128), F32),
            pltpu.VMEM((2, 4, 16, 128), F32),
            pltpu.VMEM((4, 16, 128), F32),
            pltpu.VMEM((FLAT, 128), F32),
            pltpu.VMEM((FLAT, 128), F32),
            pltpu.VMEM((FLAT, 128), F32),
            pltpu.VMEM((8, 128), F32),
            pltpu.VMEM((1, 128), F32),
            pltpu.VMEM((16, 1, 128), F32),
            pltpu.VMEM((1, 128), F32),
            pltpu.VMEM((16, 1, 128), F32),
            pltpu.SemaphoreType.DMA((7,)),
            pltpu.SemaphoreType.DMA((2,)),
            pltpu.SemaphoreType.DMA((3, 8)),
            pltpu.SemaphoreType.DMA((3, 8)),
            pltpu.SemaphoreType.DMA((2, 16)),
            pltpu.SemaphoreType.DMA((2, 16)),
        ],
        compiler_params=pltpu.CompilerParams(
            collective_id=0, has_side_effects=True, vmem_limit_bytes=48 * 1024 * 1024
        ),
        name="step",
    )(measured.reshape(FLAT, 128), psf_taps, offsets, window_mask, forward, backward, taps_x, taps_y)
    shape = (2, PLANES, 1, 1, CORE * CORE)
    return objects.reshape(shape), images.reshape(shape), factors


def solution(mesh):
    placed = (
        P(None, None, "py", "px", None),
        P("py", "px", None, None, None),
        P("py", "px", None),
        P("py", "px"),
    )
    return jax.shard_map(
        body,
        mesh=mesh,
        in_specs=placed,
        out_specs=(P(None, None, "py", "px", None), P(None, None, "py", "px", None), P()),
        check_vma=False,
    )
```

time: 468 us -> 58.4 us (0.12)
  blocking collectives: 280 us -> 0 us
  matrix products: 74.1 us -> 0 us
  starting transfers between devices: 55.3 us -> 0 us
  Pallas kernels: 0 us -> 48.6 us
  waiting for transfers between devices: 19 us -> 0 us
  other arithmetic: 10.9 us -> 0 us
  between operations: 9.35 us -> 0.66 us
  local copies, waits for them, and re-layouts: 14.9 us -> 8.79 us
    psum x3 -> x0, blocking collectives: 280 us -> none  [the longest x1 102 us: body(): beta_terms = lax.psum((third_sq, third_cross, third_tail), ('py', 'px'))]
    dot_general x46 -> x0, matrix products: 74.1 us -> none  [product(): return jnp.einsum(form, table, values, preferred_element_type=jnp.float32)]
    ppermute x16 -> x0, starting transfers between devices: 55.3 us -> none  [the longest x8 39.4 us: padded_2(): before = lax.ppermute(last, axis, up)]
    pallas_call x0 -> x1, Pallas kernels: none -> 48.6 us  [body(): pl.pallas_call(functools.partial(kernel, ny, nx), out_shape=(flat, flat,...]
    ppermute x16 -> x0, waiting for transfers between devices: 19 us -> none  [the longest x8 13.1 us: padded_2(): after = lax.ppermute(leading, axis, down)]
    convert_element_type x10 -> x0, local copies, waits for them, and re-layouts: 4.89 us -> none  [complex_axis(): return (real_out.astype(jnp.bfloat16), imag_out.astype(jnp.bfloat16))]
  transfers between devices with their start and end apart: 16 -> 0, of which waited for: 8 -> 0; matrix products, arithmetic and copies ran while one was open for 4% -> 0% of each run, Pallas kernels for 0% -> 0%
where the time goes in v1:
time: 58.4 us; the launch traced here: 58 us
  Pallas kernels  48.6 us (83%)
  local copies, waits for them, and re-layouts  8.79 us (15%)
  between operations  0.66 us (1%)
    pallas_call x1, Pallas kernels, body(): pl.pallas_call(functools.partial(kernel, ny, nx), out_shape=(flat, flat,...  48.6 us
    unnamed x19, local copies, waits for them, and re-layouts  8.79 us

profile of v1, /device:TPU:1, one launch (start us, length us, event | category | flops | bytes accessed | tf_op | source)
XLA Modules:
  0.0 58.0 jit_solution(15671718021611994074)
XLA Ops:
  0.6 0.0 copy-start.7
  0.6 0.6 %copy-done.7 = s32[1,1,2]{2,1,0:T(1,128)S(1)} copy-done((s32[1,1,2]{2,1,0:T(1,128)S(1)}, s32[1,1,2]{2,1,0:T(1,128)}, u32[]{:S(2)}) %copy-start.7) | copy-done | bytes 32
  1.3 0.0 copy-start
  1.3 0.9 %copy-done = bf16[1,1,32,32,32]{4,3,2,1,0:T(8,128)(2,1)S(1)} copy-done((bf16[1,1,32,32,32]{4,3,2,1,0:T(8,128)(2,1)S(1)}, bf16[1,1,32,32,32]{4,3,2,1,0:T(8,128)(2,1)}, u32[]{:S(2)}) %copy-start) | copy-done | bytes 65560
  2.2 0.0 copy-start.1
  2.2 0.9 %copy-done.1 = f32[2,2,1,1,12544]{4,3,2,1,0:T(1,128)S(1)} copy-done((f32[2,2,1,1,12544]{4,3,2,1,0:T(1,128)S(1)}, f32[2,2,1,1,12544]{4,3,2,1,0:T(1,128)}, u32[]{:S(2)}) %copy-start.1) | copy-done | bytes 200728
  3.2 0.0 copy-start.2
  3.2 0.9 %copy-done.2 = bf16[256,256]{1,0:T(8,128)(2,1)S(1)} copy-done((bf16[256,256]{1,0:T(8,128)(2,1)S(1)}, bf16[256,256]{1,0:T(8,128)(2,1)}, u32[]{:S(2)}) %copy-start.2) | copy-done | bytes 131096
  4.1 0.0 copy-start.3
  4.1 0.9 %copy-done.3 = bf16[256,256]{1,0:T(8,128)(2,1)S(1)} copy-done((bf16[256,256]{1,0:T(8,128)(2,1)S(1)}, bf16[256,256]{1,0:T(8,128)(2,1)}, u32[]{:S(2)}) %copy-start.3) | copy-done | bytes 131096
  5.0 0.0 copy-start.4
  5.0 0.8 %copy-done.4 = s32[128,128]{1,0:T(8,128)S(1)} copy-done((s32[128,128]{1,0:T(8,128)S(1)}, s32[128,128]{1,0:T(8,128)}, u32[]{:S(2)}) %copy-start.4) | copy-done | bytes 65560
  5.8 0.0 copy-start.5
  5.8 0.8 %copy-done.5 = bf16[256,128]{1,0:T(8,128)(2,1)S(1)} copy-done((bf16[256,128]{1,0:T(8,128)(2,1)S(1)}, bf16[256,128]{1,0:T(8,128)(2,1)}, u32[]{:S(2)}) %copy-start.5) | copy-done | bytes 65560
  6.7 0.0 copy-start.6
  6.7 0.8 %copy-done.6 = bf16[64,256]{1,0:T(8,128)(2,1)S(1)} copy-done((bf16[64,256]{1,0:T(8,128)(2,1)S(1)}, bf16[64,256]{1,0:T(8,128)(2,1)}, u32[]{:S(2)}) %copy-start.6) | copy-done | bytes 32792
  7.4 48.6 %step.1 = (f32[392,128]{1,0:T(8,128)S(1)}, f32[392,128]{1,0:T(8,128)S(1)}, f32[3,2,2]{2,1,0:T(2,128)S(1)}) custom-call(f32[392,128]{1,0:T(8,128)S(1)} %bitcast.3, bf16[1,1,32,32,32]{4,3,2,1,0:T(8,128)(2,1)S(1)} %copy-done, s32[1,1,2]{2,1,0:T(1,128)S(1)} %copy-done.7, s32[128,128]{1,0:T(8,128)S(1)} %copy-done.4, bf16[256,256]{1,0:T(8,128)(2,1)S(1)} %copy-done.3, ...), custom_call_target="tpu_custom_call" | custom-call | tf_op jit(solution)/shard_map/step/pallas_call | solution.py:485
  56.0 0.7 %copy.13 = f32[3,2,2]{0,2,1:T(2,128)} copy(f32[3,2,2]{2,1,0:T(2,128)S(1)} %get-tuple-element.11) | data formatting | bytes 96
  56.7 0.7 %copy.16 = f32[2,2,1,1,12544]{4,3,2,1,0:T(1,128)} copy(f32[2,2,1,1,12544]{4,3,2,1,0:T(1,128)S(1)} %bitcast.5) | data formatting | bytes 401408
  57.4 0.7 %copy.17 = f32[2,2,1,1,12544]{4,3,2,1,0:T(1,128)} copy(f32[2,2,1,1,12544]{4,3,2,1,0:T(1,128)S(1)} %bitcast.4) | data formatting | bytes 401408
Async XLA Ops:
  0.6 0.7 %copy-start.7 = (s32[1,1,2]{2,1,0:T(1,128)S(1)}, s32[1,1,2]{2,1,0:T(1,128)}, u32[]{:S(2)}) copy-start(s32[1,1,2]{2,1,0:T(1,128)} %offsets.1) | copy-start | bytes 28
  1.3 0.9 %copy-start = (bf16[1,1,32,32,32]{4,3,2,1,0:T(8,128)(2,1)S(1)}, bf16[1,1,32,32,32]{4,3,2,1,0:T(8,128)(2,1)}, u32[]{:S(2)}) copy-start(bf16[1,1,32,32,32]{4,3,2,1,0:T(8,128)(2,1)} %taps_hbm.1) | copy-start | bytes 196612
  2.2 0.9 %copy-start.1 = (f32[2,2,1,1,12544]{4,3,2,1,0:T(1,128)S(1)}, f32[2,2,1,1,12544]{4,3,2,1,0:T(1,128)}, u32[]{:S(2)}) copy-start(f32[2,2,1,1,12544]{4,3,2,1,0:T(1,128)} %param.8) | copy-start | bytes 602116
  3.2 0.9 %copy-start.2 = (bf16[256,256]{1,0:T(8,128)(2,1)S(1)}, bf16[256,256]{1,0:T(8,128)(2,1)}, u32[]{:S(2)}) copy-start(bf16[256,256]{1,0:T(8,128)(2,1)} %constant.9.clone.backward_hbm) | copy-start | bytes 393220
  4.1 0.9 %copy-start.3 = (bf16[256,256]{1,0:T(8,128)(2,1)S(1)}, bf16[256,256]{1,0:T(8,128)(2,1)}, u32[]{:S(2)}) copy-start(bf16[256,256]{1,0:T(8,128)(2,1)} %constant.8.clone.forward_hbm) | copy-start | bytes 393220
  5.0 0.8 %copy-start.4 = (s32[128,128]{1,0:T(8,128)S(1)}, s32[128,128]{1,0:T(8,128)}, u32[]{:S(2)}) copy-start(s32[128,128]{1,0:T(8,128)} %mask_hbm.1) | copy-start | bytes 196612
  5.8 0.8 %copy-start.5 = (bf16[256,128]{1,0:T(8,128)(2,1)S(1)}, bf16[256,128]{1,0:T(8,128)(2,1)}, u32[]{:S(2)}) copy-start(bf16[256,128]{1,0:T(8,128)(2,1)} %constant.11.clone.taps_y_hbm) | copy-start | bytes 196612
  6.7 0.8 %copy-start.6 = (bf16[64,256]{1,0:T(8,128)(2,1)S(1)}, bf16[64,256]{1,0:T(8,128)(2,1)}, u32[]{:S(2)}) copy-start(bf16[64,256]{1,0:T(8,128)(2,1)} %constant.10.clone.taps_x_hbm) | copy-start | bytes 98308

commit v2 on v1

--- a/solution.py
+++ b/solution.py
@@ -181,32 +181,15 @@
 
 def kernel(
     ny, nx,
-    measured_hbm, taps_hbm, offsets, mask_hbm, forward_hbm, backward_hbm, taps_x_hbm, taps_y_hbm,
-    object_hbm, image_hbm, factors_ref,
-    measured, taps, mask, forward_ref, backward_ref, taps_x, taps_y,
+    measured_hbm, taps_hbm, offsets_hbm, mask_hbm, forward_hbm, backward_hbm, taps_x_hbm, taps_y_hbm,
+    object_ref, image_ref, factors_ref,
+    measured, offsets, taps, mask, forward_ref, backward_ref, taps_x, taps_y,
     spectrum_ref, planes, packed, turned, row8, col_in, corner8, row16, corner16,
-    object_flat, forward_flat, image_flat, grid_ref,
+    object_flat, forward_flat,
     one_out, one_in, two_out, two_in,
-    load_sem, store_sem, send_sem, recv_sem, sum_send, sum_recv,
+    load_sem, send_sem, recv_sem, sum_send, sum_recv,
 ):
     py, px = lax.axis_index("py"), lax.axis_index("px")
-    loads = [
-        pltpu.make_async_copy(source, target, load_sem.at[i])
-        for i, (source, target) in enumerate(
-            [
-                (measured_hbm, measured),
-                (taps_hbm.at[0, 0, pl.ds(TAP, 3)], taps),
-                (taps_x_hbm, taps_x),
-                (taps_y_hbm, taps_y),
-                (mask_hbm, mask),
-                (forward_hbm, forward_ref),
-                (backward_hbm, backward_ref),
-            ]
-        )
-    ]
-    for load in loads:
-        load.start()
-
     row, high, column = px // 8, lax.rem(px // 4, 2), lax.rem(px, 4)
     place_one, place_two = high * ny + py, row * 4 + column
 
@@ -243,6 +226,24 @@
         for to in (partner_one(step), partner_two(step)):
             pl.semaphore_signal(barrier, inc=1, device_id=to, device_id_type=pl.DeviceIdType.MESH)
             greeted += 1
+
+    loads = [
+        pltpu.make_async_copy(source, target, load_sem.at[i])
+        for i, (source, target) in enumerate(
+            [
+                (measured_hbm, measured),
+                (taps_hbm.at[0, 0, pl.ds(TAP, 3)], taps),
+                (taps_x_hbm, taps_x),
+                (taps_y_hbm, taps_y),
+                (offsets_hbm, offsets),
+                (mask_hbm, mask),
+                (forward_hbm, forward_ref),
+                (backward_hbm, backward_ref),
+            ]
+        )
+    ]
+    for load in loads:
+        load.start()
 
     lane = lax.broadcasted_iota(jnp.int32, (PATCH, 128), 1)
     line = lax.broadcasted_iota(jnp.int32, (PATCH, 128), 0)
@@ -272,7 +273,7 @@
     pl.semaphore_wait(barrier, greeted)
     first.start()
 
-    for load in loads[1:4]:
+    for load in loads[1:5]:
         load.wait()
     shift_y, shift_x = offsets[0, 0, 0], offsets[0, 0, 1]
     pick_x = (
@@ -296,7 +297,7 @@
     )
     spectrum_ref[...] = mm(taps_y[...], kx) * F32(1.0 / (PATCH * PATCH))
 
-    for load in loads[4:]:
+    for load in loads[5:]:
         load.wait()
     weight = mask[...].astype(F32)
 
@@ -452,43 +453,48 @@
     v_one, v_two = object_flat[one, :], object_flat[two, :]
     f_one, f_two = forward_flat[one, :], forward_flat[two, :]
     m_one, m_two = measured[one, :], measured[two, :]
-    object_flat[one, :] = t00 * v_one
-    object_flat[two, :] = t01 * v_one + t11 * v_two
-    image_flat[one, :] = i0[0] * f_one - i0[2] * m_one - i0[3] * m_two
-    image_flat[two, :] = i1[0] * f_one + i1[1] * f_two - i1[2] * m_one - i1[3] * m_two
-    stores = [
-        pltpu.make_async_copy(object_flat, object_hbm, store_sem.at[0]),
-        pltpu.make_async_copy(image_flat, image_hbm, store_sem.at[1]),
-    ]
-    for store in stores:
-        store.start()
-    which = lax.broadcasted_iota(jnp.int32, (3, 2, 2), 0)
-    down = lax.broadcasted_iota(jnp.int32, (3, 2, 2), 1)
-    across = lax.broadcasted_iota(jnp.int32, (3, 2, 2), 2)
-    factors = jnp.zeros((3, 2, 2), F32)
+    object_ref[one, :] = t00 * v_one
+    object_ref[two, :] = t01 * v_one + t11 * v_two
+    image_ref[one, :] = i0[0] * f_one - i0[2] * m_one - i0[3] * m_two
+    image_ref[two, :] = i1[0] * f_one + i1[1] * f_two - i1[2] * m_one - i1[3] * m_two
+    down = lax.broadcasted_iota(jnp.int32, (2, 2, 3), 0)
+    across = lax.broadcasted_iota(jnp.int32, (2, 2, 3), 1)
+    which = lax.broadcasted_iota(jnp.int32, (2, 2, 3), 2)
+    factors = jnp.zeros((2, 2, 3), F32)
     for i, triple in enumerate(((a, b, c), (alpha, beta, gamma), (rho, sigma, tau))):
         for (r, k), value in zip(((0, 0), (0, 1), (1, 1)), triple):
             here = (which == i) & (down == r) & (across == k)
             factors = jnp.where(here, value.reshape(1, 1, 1), factors)
     factors_ref[...] = factors
-    for store in stores:
-        store.wait()
+
+
+def store(object_vmem, image_vmem, factors_vmem, object_hbm, image_hbm, factors_hbm, sem):
+    copies = [
+        pltpu.make_async_copy(source, target, sem.at[i])
+        for i, (source, target) in enumerate(
+            ((object_vmem, object_hbm), (image_vmem, image_hbm), (factors_vmem, factors_hbm))
+        )
+    ]
+    for copy in copies:
+        copy.start()
+    for copy in copies:
+        copy.wait()
 
 
 def body(measured, psf_taps, offsets, window_mask):
     ny, nx = lax.axis_size("py"), lax.axis_size("px")
-    any_space = pl.BlockSpec(memory_space=pl.ANY)
+    hbm = pl.BlockSpec(memory_space=pltpu.HBM)
     vmem = pl.BlockSpec(memory_space=pltpu.VMEM)
-    smem = pl.BlockSpec(memory_space=pltpu.SMEM)
-    flat = jax.ShapeDtypeStruct((FLAT, 128), F32)
-    forward, backward, taps_x, taps_y = tables()
-    objects, images, factors = pl.pallas_call(
+    operands = [measured.reshape(FLAT, 128), psf_taps, offsets, window_mask, *tables()]
+    operands = [pltpu.with_memory_space_constraint(operand, pltpu.HBM) for operand in operands]
+    results = pl.pallas_call(
         functools.partial(kernel, ny, nx),
-        out_shape=(flat, flat, jax.ShapeDtypeStruct((3, 2, 2), F32)),
-        in_specs=[any_space, any_space, smem, any_space, any_space, any_space, any_space, any_space],
-        out_specs=(any_space, any_space, vmem),
+        out_shape=(pltpu.VMEM((FLAT, 128), F32), pltpu.VMEM((FLAT, 128), F32), pltpu.VMEM((2, 2, 3), F32)),
+        in_specs=[hbm] * 8,
+        out_specs=(vmem, vmem, vmem),
         scratch_shapes=[
             pltpu.VMEM((FLAT, 128), F32),
+            pltpu.SMEM((1, 1, 2), jnp.int32),
             pltpu.VMEM((3, KERNEL, KERNEL), BF16),
             pltpu.VMEM((PATCH, PATCH), jnp.int32),
             pltpu.VMEM((256, 256), BF16),
@@ -506,14 +512,11 @@
             pltpu.VMEM((4, 16, 128), F32),
             pltpu.VMEM((FLAT, 128), F32),
             pltpu.VMEM((FLAT, 128), F32),
-            pltpu.VMEM((FLAT, 128), F32),
-            pltpu.VMEM((8, 128), F32),
             pltpu.VMEM((1, 128), F32),
             pltpu.VMEM((16, 1, 128), F32),
             pltpu.VMEM((1, 128), F32),
             pltpu.VMEM((16, 1, 128), F32),
-            pltpu.SemaphoreType.DMA((7,)),
-            pltpu.SemaphoreType.DMA((2,)),
+            pltpu.SemaphoreType.DMA((8,)),
             pltpu.SemaphoreType.DMA((3, 8)),
             pltpu.SemaphoreType.DMA((3, 8)),
             pltpu.SemaphoreType.DMA((2, 16)),
@@ -523,9 +526,18 @@
             collective_id=0, has_side_effects=True, vmem_limit_bytes=48 * 1024 * 1024
         ),
         name="step",
-    )(measured.reshape(FLAT, 128), psf_taps, offsets, window_mask, forward, backward, taps_x, taps_y)
+    )(*operands)
+    results = [pltpu.with_memory_space_constraint(result, pltpu.VMEM) for result in results]
+    objects, images, factors = pl.pallas_call(
+        store,
+        out_shape=(pltpu.HBM((FLAT, 128), F32), pltpu.HBM((FLAT, 128), F32), pltpu.HBM((2, 2, 3), F32)),
+        in_specs=[vmem] * 3,
+        out_specs=(hbm, hbm, hbm),
+        scratch_shapes=[pltpu.SemaphoreType.DMA((3,))],
+        name="store",
+    )(*results)
     shape = (2, PLANES, 1, 1, CORE * CORE)
-    return objects.reshape(shape), images.reshape(shape), factors
+    return objects.reshape(shape), images.reshape(shape), factors.transpose(2, 0, 1)
 
 
 def solution(mesh):

time: 58.4 us -> 48.3 us (0.83)
  local copies, waits for them, and re-layouts: 8.79 us -> 0 us
  Pallas kernels: 48.6 us -> 47.5 us
    unnamed x19 -> x0, local copies, waits for them, and re-layouts: 8.79 us -> none
    pallas_call x1 -> x2, Pallas kernels: 48.6 us -> 47.5 us  [the longest x1 46.7 us: body(): pl.pallas_call(functools.partial(kernel, ny, nx), out_shape=(pltpu.VMEM((...]
where the time goes in v2:
time: 48.3 us; the launch traced here: 48.2 us
  Pallas kernels  47.5 us (98%)
  between operations  0.64 us (1%)
    pallas_call x1, Pallas kernels, body(): pl.pallas_call(functools.partial(kernel, ny, nx), out_shape=(pltpu.VMEM((...  46.7 us

profile of v2, /device:TPU:1, one launch (start us, length us, event | category | flops | bytes accessed | tf_op | source)
XLA Modules:
  0.0 48.2 jit_solution(15803685850309446551)
XLA Ops:
  0.6 46.7 %step.1 = (f32[392,128]{1,0:T(8,128)S(1)}, f32[392,128]{1,0:T(8,128)S(1)}, f32[2,2,3]{2,1,0:T(2,128)S(1)}) custom-call(f32[392,128]{1,0:T(8,128)} %bitcast.4, bf16[1,1,32,32,32]{4,3,2,1,0:T(8,128)(2,1)} %taps_hbm.1, s32[1,1,2]{2,1,0:T(1,128)} %offsets_hbm.1, s32[128,128]{1,0:T(8,128)} %mask_hbm.1, bf16[256,256]{1,0:T(8,128)(2,1)} %constant.8.clone.forward_hbm, ...), custom_call_target="tpu_custom_call" | custom-call | tf_op jit(solution)/shard_map/step/pallas_call | solution.py:490
  47.4 0.8 %store.1 = (f32[392,128]{1,0:T(8,128)}, f32[392,128]{1,0:T(8,128)}, f32[2,2,3]{2,1,0:T(2,128)}) custom-call(f32[392,128]{1,0:T(8,128)S(1)} %get-tuple-element.9.object_vmem, f32[392,128]{1,0:T(8,128)S(1)} %get-tuple-element.10.image_vmem, f32[2,2,3]{2,1,0:T(2,128)S(1)} %get-tuple-element.11.factors_vmem), custom_call_target="tpu_custom_call" | custom-call | tf_op jit(solution)/shard_map/store/pallas_call | solution.py:531

commit v3 on v2

--- a/solution.py
+++ b/solution.py
@@ -55,17 +55,18 @@
         py, px = lax.axis_index("py"), lax.axis_index("px")
         up, down = lax.rem(py + ny - 1, ny), lax.rem(py + 1, ny)
         left, right = lax.rem(px + nx - 1, nx), lax.rem(px + 1, nx)
+        has_up, has_down, has_left, has_right = py > 0, py < ny - 1, px > 0, px < nx - 1
         top, bottom = pl.ds(rows[0], height), pl.ds(rows[1], height)
         (left_from, left_to), (right_from, right_to) = cols
         plan = [
-            (planes.at[:, top, :], row_in.at[1], up, px),
-            (planes.at[:, bottom, :], row_in.at[0], down, px),
-            (turned.at[:, pl.ds(left_from, height), :], col_in.at[:, pl.ds(left_to, height), :], py, left),
-            (turned.at[:, pl.ds(right_from, height), :], col_in.at[:, pl.ds(right_to, height), :], py, right),
-            (packed.at[top, :], corner_in.at[3], up, left),
-            (packed.at[top, :], corner_in.at[2], up, right),
-            (packed.at[bottom, :], corner_in.at[1], down, left),
-            (packed.at[bottom, :], corner_in.at[0], down, right),
+            (planes.at[:, top, :], row_in.at[1], up, px, has_up),
+            (planes.at[:, bottom, :], row_in.at[0], down, px, has_down),
+            (turned.at[:, pl.ds(left_from, height), :], col_in.at[:, pl.ds(left_to, height), :], py, left, has_left),
+            (turned.at[:, pl.ds(right_from, height), :], col_in.at[:, pl.ds(right_to, height), :], py, right, has_right),
+            (packed.at[top, :], corner_in.at[3], up, left, has_up & has_left),
+            (packed.at[top, :], corner_in.at[2], up, right, has_up & has_right),
+            (packed.at[bottom, :], corner_in.at[1], down, left, has_down & has_left),
+            (packed.at[bottom, :], corner_in.at[0], down, right, has_down & has_right),
         ]
         self.copies = [
             pltpu.make_async_remote_copy(
@@ -76,28 +77,30 @@
                 device_id={"py": to_y, "px": to_x},
                 device_id_type=pl.DeviceIdType.MESH,
             )
-            for i, (source, target, to_y, to_x) in enumerate(plan)
+            for i, (source, target, to_y, to_x, _) in enumerate(plan)
         ]
+        self.there = [there for *_, there in plan]
+        self.back = [self.there[i] for i in (1, 0, 3, 2, 7, 6, 5, 4)]
 
     def start(self):
         lane = lax.broadcasted_iota(jnp.int32, (PATCH, 128), 1)
-        for copy in self.copies[:2]:
-            copy.start()
         packed = roll(self.planes[0], 16)
         for m in range(1, 2 * PLANES):
             packed = jnp.where(lane >= 32 * m, roll(self.planes[m], 16 + 32 * m), packed)
         self.packed[...] = packed
+        for i in range(4, 8):
+            pl.when(self.there[i])(self.copies[i].start)
         self.turned[...] = packed.T.reshape(2 * PLANES, 32, PATCH)
-        for copy in self.copies[2:]:
-            copy.start()
+        for i in (2, 3, 0, 1):
+            pl.when(self.there[i])(self.copies[i].start)
 
     def wait_recv(self):
-        for copy in self.copies:
-            copy.wait_recv()
+        for copy, there in zip(self.copies, self.back):
+            pl.when(there)(copy.wait_recv)
 
     def wait_send(self):
-        for copy in self.copies:
-            copy.wait_send()
+        for copy, there in zip(self.copies, self.there):
+            pl.when(there)(copy.wait_send)
 
     def sides(self):
         columns = self.col_in[...].reshape(4 * 32, PATCH).T
@@ -215,17 +218,18 @@
         turned=turned.at[2], row_in=row8.at[1], col_in=col_in.at[2], corner_in=corner8.at[1],
     )
     barrier = pltpu.get_barrier_semaphore()
-    greeted = 0
-    for dy in (ny - 1, 0, 1):
-        for dx in (nx - 1, 0, 1):
-            if dy or dx:
+    has_up, has_down, has_left, has_right = py > 0, py < ny - 1, px > 0, px < nx - 1
+    greeted = jnp.int32(30)
+    for dx, has_x in ((nx - 1, has_left), (1, has_right), (0, None)):
+        for dy, has_y in ((ny - 1, has_up), (1, has_down), (0, None)):
+            if dx or dy:
+                there = has_x if has_y is None else has_y if has_x is None else has_x & has_y
                 to = {"py": lax.rem(py + dy, ny), "px": lax.rem(px + dx, nx)}
-                pl.semaphore_signal(barrier, inc=1, device_id=to, device_id_type=pl.DeviceIdType.MESH)
-                greeted += 1
-    for step in range(1, 16):
-        for to in (partner_one(step), partner_two(step)):
-            pl.semaphore_signal(barrier, inc=1, device_id=to, device_id_type=pl.DeviceIdType.MESH)
-            greeted += 1
+                greeted += there.astype(jnp.int32)
+
+                @pl.when(there)
+                def _(to=to):
+                    pl.semaphore_signal(barrier, inc=1, device_id=to, device_id_type=pl.DeviceIdType.MESH)
 
     loads = [
         pltpu.make_async_copy(source, target, load_sem.at[i])
@@ -245,10 +249,13 @@
     for load in loads:
         load.start()
 
+    for step in range(1, 16):
+        for to in (partner_one(step), partner_two(step)):
+            pl.semaphore_signal(barrier, inc=1, device_id=to, device_id_type=pl.DeviceIdType.MESH)
+
     lane = lax.broadcasted_iota(jnp.int32, (PATCH, 128), 1)
     line = lax.broadcasted_iota(jnp.int32, (PATCH, 128), 0)
     owned_lane = (lane >= HALF) & (lane < PATCH - HALF)
-    has_up, has_down, has_left, has_right = py > 0, py < ny - 1, px > 0, px < nx - 1
     low_y, high_y = jnp.where(has_up, 0, HALF), jnp.where(has_down, PATCH, PATCH - HALF)
     low_x, high_x = jnp.where(has_left, 0, HALF), jnp.where(has_right, PATCH, PATCH - HALF)
     inside = (line >= low_y) & (line < high_y) & (lane >= low_x) & (lane < high_x)

time: 48.3 us -> 45.6 us (0.944)
  Pallas kernels: 47.5 us -> 44.8 us
    pallas_call x1, Pallas kernels: 46.7 us -> 44 us  [body(): pl.pallas_call(functools.partial(kernel, ny, nx), out_shape=(pltpu.VMEM((...]
where the time goes in v3:
time: 45.6 us; the launch traced here: 45.5 us
  Pallas kernels  44.8 us (98%)
  between operations  0.64 us (1%)
    pallas_call x1, Pallas kernels, body(): pl.pallas_call(functools.partial(kernel, ny, nx), out_shape=(pltpu.VMEM((...  44 us

profile of v3, /device:TPU:1, one launch (start us, length us, event | category | flops | bytes accessed | tf_op | source)
XLA Modules:
  0.0 45.5 jit_solution(8069961370177707259)
XLA Ops:
  0.6 44.0 %step.1 = (f32[392,128]{1,0:T(8,128)S(1)}, f32[392,128]{1,0:T(8,128)S(1)}, f32[2,2,3]{2,1,0:T(2,128)S(1)}) custom-call(f32[392,128]{1,0:T(8,128)} %bitcast.4, bf16[1,1,32,32,32]{4,3,2,1,0:T(8,128)(2,1)} %taps_hbm.1, s32[1,1,2]{2,1,0:T(1,128)} %offsets_hbm.1, s32[128,128]{1,0:T(8,128)} %mask_hbm.1, bf16[256,256]{1,0:T(8,128)(2,1)} %constant.8.clone.forward_hbm, ...), custom_call_target="tpu_custom_call" | custom-call | tf_op jit(solution)/shard_map/step/pallas_call | solution.py:497
  44.7 0.8 %store.1 = (f32[392,128]{1,0:T(8,128)}, f32[392,128]{1,0:T(8,128)}, f32[2,2,3]{2,1,0:T(2,128)}) custom-call(f32[392,128]{1,0:T(8,128)S(1)} %get-tuple-element.9.object_vmem, f32[392,128]{1,0:T(8,128)S(1)} %get-tuple-element.10.image_vmem, f32[2,2,3]{2,1,0:T(2,128)S(1)} %get-tuple-element.11.factors_vmem), custom_call_target="tpu_custom_call" | custom-call | tf_op jit(solution)/shard_map/store/pallas_call | solution.py:538

commit v4 on v3

--- a/solution.py
+++ b/solution.py
@@ -48,25 +48,25 @@
 
 
 class Exchange:
-    def __init__(self, index, ny, nx, height, rows, cols, planes, packed, turned, row_in, col_in, corner_in, send, recv):
-        self.index, self.height = index, height
-        self.planes, self.packed, self.turned = planes, packed, turned
-        self.row_in, self.col_in, self.corner_in = row_in, col_in, corner_in
+    def __init__(self, index, ny, nx, height, rows, cols_out, cols_in, outs, ins, send, recv):
+        self.height, self.rows, self.cols_out, self.cols_in = height, rows, cols_out, cols_in
+        self.row_out, self.col_out, self.corner_out = (ref.at[index] for ref in outs)
+        self.row_in, self.col_in, self.corner_in = (ref.at[index] for ref in ins)
         py, px = lax.axis_index("py"), lax.axis_index("px")
         up, down = lax.rem(py + ny - 1, ny), lax.rem(py + 1, ny)
         left, right = lax.rem(px + nx - 1, nx), lax.rem(px + 1, nx)
         has_up, has_down, has_left, has_right = py > 0, py < ny - 1, px > 0, px < nx - 1
-        top, bottom = pl.ds(rows[0], height), pl.ds(rows[1], height)
-        (left_from, left_to), (right_from, right_to) = cols
+        strip = pl.ds(0, 4 * height)
+        top, bottom = (pl.ds(0, 16), pl.ds(16, 16)) if height == 16 else (pl.ds(0, 16), pl.ds(0, 16))
         plan = [
-            (planes.at[:, top, :], row_in.at[1], up, px, has_up),
-            (planes.at[:, bottom, :], row_in.at[0], down, px, has_down),
-            (turned.at[:, pl.ds(left_from, height), :], col_in.at[:, pl.ds(left_to, height), :], py, left, has_left),
-            (turned.at[:, pl.ds(right_from, height), :], col_in.at[:, pl.ds(right_to, height), :], py, right, has_right),
-            (packed.at[top, :], corner_in.at[3], up, left, has_up & has_left),
-            (packed.at[top, :], corner_in.at[2], up, right, has_up & has_right),
-            (packed.at[bottom, :], corner_in.at[1], down, left, has_down & has_left),
-            (packed.at[bottom, :], corner_in.at[0], down, right, has_down & has_right),
+            (self.row_out.at[0, strip], self.row_in.at[1, strip], up, px, has_up),
+            (self.row_out.at[1, strip], self.row_in.at[0, strip], down, px, has_down),
+            (self.col_out.at[0, strip], self.col_in.at[1, strip], py, left, has_left),
+            (self.col_out.at[1, strip], self.col_in.at[0, strip], py, right, has_right),
+            (self.corner_out.at[top], self.corner_in.at[3], up, left, has_up & has_left),
+            (self.corner_out.at[top], self.corner_in.at[2], up, right, has_up & has_right),
+            (self.corner_out.at[bottom], self.corner_in.at[1], down, left, has_down & has_left),
+            (self.corner_out.at[bottom], self.corner_in.at[0], down, right, has_down & has_right),
         ]
         self.copies = [
             pltpu.make_async_remote_copy(
@@ -82,16 +82,31 @@
         self.there = [there for *_, there in plan]
         self.back = [self.there[i] for i in (1, 0, 3, 2, 7, 6, 5, 4)]
 
+    def pack(self, planes, starting=False):
+        def start(*which):
+            for i in which if starting else ():
+                pl.when(self.there[i])(self.copies[i].start)
+
+        lane = lax.broadcasted_iota(jnp.int32, (PATCH, 128), 1)
+        height, (top, bottom) = self.height, self.rows
+        packed = roll(planes[0], 16)
+        for m in range(1, 2 * PLANES):
+            packed = jnp.where(lane >= 32 * m, roll(planes[m], 16 + 32 * m), packed)
+        ends = jnp.concatenate([packed[top : top + height], packed[bottom : bottom + height]], axis=0)
+        self.corner_out[0 : 2 * height, :] = ends.astype(BF16)
+        start(4, 5, 6, 7)
+        turned = packed.T
+        for side, first in enumerate(self.cols_out):
+            strips = [turned[32 * m + first : 32 * m + first + height] for m in range(2 * PLANES)]
+            self.col_out[side, 0 : 4 * height, :] = jnp.concatenate(strips, axis=0).astype(BF16)
+        start(2, 3)
+        for side, first in enumerate(self.rows):
+            strips = [planes[m][first : first + height] for m in range(2 * PLANES)]
+            self.row_out[side, 0 : 4 * height, :] = jnp.concatenate(strips, axis=0).astype(BF16)
+        start(0, 1)
+
     def start(self):
-        lane = lax.broadcasted_iota(jnp.int32, (PATCH, 128), 1)
-        packed = roll(self.planes[0], 16)
-        for m in range(1, 2 * PLANES):
-            packed = jnp.where(lane >= 32 * m, roll(self.planes[m], 16 + 32 * m), packed)
-        self.packed[...] = packed
-        for i in range(4, 8):
-            pl.when(self.there[i])(self.copies[i].start)
-        self.turned[...] = packed.T.reshape(2 * PLANES, 32, PATCH)
-        for i in (2, 3, 0, 1):
+        for i in (4, 5, 6, 7, 2, 3, 0, 1):
             pl.when(self.there[i])(self.copies[i].start)
 
     def wait_recv(self):
@@ -102,26 +117,43 @@
         for copy, there in zip(self.copies, self.there):
             pl.when(there)(copy.wait_send)
 
+    def row_strips(self):
+        height = self.height
+        both = [self.row_in[side, 0 : 4 * height, :].astype(F32) for side in range(2)]
+        return [[strips[m * height : (m + 1) * height] for m in range(2 * PLANES)] for strips in both]
+
     def sides(self):
-        columns = self.col_in[...].reshape(4 * 32, PATCH).T
-        lane = lax.broadcasted_iota(jnp.int32, (self.height, 128), 1)
+        height = self.height
+        both = [self.col_in[side, 0 : 4 * height, :].astype(F32) for side in range(2)]
+        pieces = []
+        for m in range(2 * PLANES):
+            slots = [both[1][m * height : (m + 1) * height] for _ in range(32 // height)]
+            slots[self.cols_in // height] = both[0][m * height : (m + 1) * height]
+            pieces += slots
+        columns = jnp.concatenate(pieces, axis=0).T
+        lane = lax.broadcasted_iota(jnp.int32, (height, 128), 1)
         is_left = lax.rem(lane, 32) >= 16
-        upper = jnp.where(is_left, roll(self.corner_in[0], 16), roll(self.corner_in[1], -16))
-        lower = jnp.where(is_left, roll(self.corner_in[2], 16), roll(self.corner_in[3], -16))
+        corner = [self.corner_in[i].astype(F32) for i in range(4)]
+        if height == 8:
+            corner = [corner[0][8:], corner[1][8:], corner[2][:8], corner[3][:8]]
+        upper = jnp.where(is_left, roll(corner[0], 16), roll(corner[1], -16))
+        lower = jnp.where(is_left, roll(corner[2], 16), roll(corner[3], -16))
         return columns, upper, lower
 
 
-def normalised(cells):
-    s00 = sum(total(cells[0][z] * cells[0][z]) for z in range(PLANES))
-    s01 = sum(total(cells[0][z] * cells[1][z]) for z in range(PLANES))
-    s11 = sum(total(cells[1][z] * cells[1][z]) for z in range(PLANES))
+def normaliser(s00, s01, s11):
     tiny = F32(1e-30)
     q0 = lax.rsqrt(jnp.maximum(s00, tiny))
     cross = s01 * q0
     q1 = lax.rsqrt(jnp.maximum(s11 - cross * cross, s11 * F32(1e-6) + tiny))
+    return (q0, cross, q1), (1.0 / q0, cross, 1.0 / q1)
+
+
+def normalised(cells, scalars):
+    q0, cross, q1 = scalars
     first = [cells[0][z] * q0 for z in range(PLANES)]
     second = [(cells[1][z] - cross * first[z]) * q1 for z in range(PLANES)]
-    return (first, second), (1.0 / q0, cross, 1.0 / q1)
+    return first, second
 
 
 def blur(cells, spectrum, forward_ref, backward_ref, adjoint):
@@ -187,7 +219,7 @@
     measured_hbm, taps_hbm, offsets_hbm, mask_hbm, forward_hbm, backward_hbm, taps_x_hbm, taps_y_hbm,
     object_ref, image_ref, factors_ref,
     measured, offsets, taps, mask, forward_ref, backward_ref, taps_x, taps_y,
-    spectrum_ref, planes, packed, turned, row8, col_in, corner8, row16, corner16,
+    spectrum_ref, planes, row_out, col_out, corner_out, row_in, col_in, corner_in,
     object_flat, forward_flat,
     one_out, one_in, two_out, two_in,
     load_sem, send_sem, recv_sem, sum_send, sum_recv,
@@ -204,19 +236,13 @@
         at = lax.rem(place_two + step, 16)
         return {"py": py, "px": (at // 4) * 8 + high * 4 + lax.rem(at, 4)}
 
-    exchange = functools.partial(Exchange, ny=ny, nx=nx, send=send_sem, recv=recv_sem)
-    first = exchange(
-        index=0, height=8, rows=(8, 112), cols=((24, 8), (0, 16)), planes=planes.at[0], packed=packed.at[0],
-        turned=turned.at[0], row_in=row8.at[0], col_in=col_in.at[0], corner_in=corner8.at[0],
-    )
-    second = exchange(
-        index=1, height=16, rows=(0, 112), cols=((16, 0), (0, 16)), planes=planes.at[1], packed=packed.at[1],
-        turned=turned.at[1], row_in=row16, col_in=col_in.at[1], corner_in=corner16,
-    )
-    third = exchange(
-        index=2, height=8, rows=(0, 120), cols=((16, 0), (8, 24)), planes=planes.at[2], packed=packed.at[2],
-        turned=turned.at[2], row_in=row8.at[1], col_in=col_in.at[2], corner_in=corner8.at[1],
-    )
+    exchange = functools.partial(
+        Exchange, ny=ny, nx=nx, outs=(row_out, col_out, corner_out), ins=(row_in, col_in, corner_in),
+        send=send_sem, recv=recv_sem,
+    )
+    first = exchange(index=0, height=8, rows=(8, 112), cols_out=(24, 0), cols_in=16)
+    second = exchange(index=1, height=16, rows=(0, 112), cols_out=(16, 0), cols_in=16)
+    third = exchange(index=2, height=8, rows=(0, 120), cols_out=(16, 8), cols_in=24)
     barrier = pltpu.get_barrier_semaphore()
     has_up, has_down, has_left, has_right = py > 0, py < ny - 1, px > 0, px < nx - 1
     greeted = jnp.int32(30)
@@ -277,6 +303,7 @@
                 both = jnp.where(lane14 >= 128 - 16 * k, low_part, high_part)
             planes[0, m, pl.ds(HALF + k, 14, stride=8), :] = roll(both, 16 * k + HALF)
 
+    first.pack([planes[0, m] for m in range(4)])
     pl.semaphore_wait(barrier, greeted)
     first.start()
 
@@ -320,45 +347,49 @@
 
     sums = grams(own_m, own_m, ((0, 0), (0, 1), (1, 1)))
 
+    def scalars_of(tiles):
+        return normaliser(*(total(values) for values in tiles))
+
+    scalars, factor = scalars_of(sums)
     first.wait_recv()
     columns, upper, lower = first.sides()
+    up_rows, down_rows = first.row_strips()
     columns = jnp.concatenate([upper, columns[owned], lower], axis=0)
     window = [[None, None], [None, None]]
     for m in range(4):
-        centre = jnp.concatenate([row8[0, 0, m], planes[0, m, owned, :], row8[0, 1, m]], axis=0)
+        centre = jnp.concatenate([up_rows[m], planes[0, m, owned, :], down_rows[m]], axis=0)
         cells = jnp.where(owned_lane, centre, roll(columns, -16 - 32 * m))
         window[m // 2][m % 2] = jnp.where(inside, cells, 0.0)
-    unit, factor = normalised(window)
-    result = restored(blur(unit, spectrum_ref[...], forward_ref, backward_ref, True), factor)
+    result = restored(blur(normalised(window, scalars), spectrum_ref[...], forward_ref, backward_ref, True), factor)
+    result = [result[m // 2][m % 2] * weight for m in range(4)]
+    second.pack(result, starting=True)
     for m in range(4):
-        planes[1, m] = result[m // 2][m % 2] * weight
-    second.start()
-    first.wait_send()
+        planes[1, m] = result[m]
+    pairs = ((0, 0), (0, 1), (1, 1))
+    scalars, factor = scalars_of(grams((result[:2], result[2:]), (result[:2], result[2:]), pairs))
 
     second.wait_recv()
     columns, upper, lower = second.sides()
+    up_rows, down_rows = second.row_strips()
     upper, lower = jnp.where(has_up, upper, 0.0), jnp.where(has_down, lower, 0.0)
     columns = jnp.concatenate([columns[:16] + upper, columns[16:112], columns[112:] + lower], axis=0)
     edge_lane = ((lane < 16) & has_left) | ((lane >= 112) & has_right)
-    second.wait_send()
     window = [[None, None], [None, None]]
-    own_v = [[None, None], [None, None]]
     keep = jnp.where(inside, weight, 0.0)
     for m in range(4):
         cells = planes[1, m]
-        up_rows = jnp.where(has_up, row16[0, m], 0.0)
-        down_rows = jnp.where(has_down, row16[1, m], 0.0)
-        cells = jnp.concatenate([cells[:16] + up_rows, cells[16:112], cells[112:] + down_rows], axis=0)
+        above, below = jnp.where(has_up, up_rows[m], 0.0), jnp.where(has_down, down_rows[m], 0.0)
+        cells = jnp.concatenate([cells[:16] + above, cells[16:112], cells[112:] + below], axis=0)
         cells = cells + jnp.where(edge_lane, roll(columns, -16 - 32 * m), 0.0)
         planes[1, m] = cells
-        own_v[m // 2][m % 2] = jnp.where(owned_core, cells[owned], 0.0)
         window[m // 2][m % 2] = cells * keep
-    sums += grams(own_v, own_v, ((0, 0), (0, 1), (1, 1)))
-    unit, factor = normalised(window)
-    result = restored(blur(unit, spectrum_ref[...], forward_ref, backward_ref, False), factor)
+    result = restored(blur(normalised(window, scalars), spectrum_ref[...], forward_ref, backward_ref, False), factor)
+    result = [result[m // 2][m % 2] for m in range(4)]
+    third.pack(result, starting=True)
     for m in range(4):
-        planes[2, m] = result[m // 2][m % 2]
-    third.start()
+        planes[2, m] = result[m]
+    own_v = [[jnp.where(owned_core, planes[1, 2 * k + z, owned, :], 0.0) for z in range(PLANES)] for k in range(2)]
+    sums += grams(own_v, own_v, pairs)
 
     def to_flat(source, target):
         for m in range(4):
@@ -373,14 +404,13 @@
     columns, upper, lower = third.sides()
     upper, lower = jnp.where(has_up, upper, 0.0), jnp.where(has_down, lower, 0.0)
     columns = jnp.concatenate([columns[:8], columns[8:16] + upper, columns[16:112], columns[112:120] + lower, columns[120:]], axis=0)
-    third.wait_send()
+    up_rows, down_rows = third.row_strips()
     edge_lane = ((lane >= 8) & (lane < 16) & has_left) | ((lane >= 112) & (lane < 120) & has_right)
     own_f = [[None, None], [None, None]]
     for m in range(4):
         cells = planes[2, m]
-        up_rows = jnp.where(has_up, row8[1, 0, m], 0.0)
-        down_rows = jnp.where(has_down, row8[1, 1, m], 0.0)
-        cells = jnp.concatenate([cells[8:16] + up_rows, cells[16:112], cells[112:120] + down_rows], axis=0)
+        above, below = jnp.where(has_up, up_rows[m], 0.0), jnp.where(has_down, down_rows[m], 0.0)
+        cells = jnp.concatenate([cells[8:16] + above, cells[16:112], cells[112:120] + below], axis=0)
         cells = cells + jnp.where(edge_lane[owned], roll(columns[owned], -16 - 32 * m), 0.0)
         cells = jnp.where(owned_core, cells, 0.0)
         planes[2, m, owned, :] = cells
@@ -417,9 +447,14 @@
     copies = all_sum(mine, one_out, one_in, place_one, partner_one, 0)
     to_flat(lambda m, rows: planes[2, m, rows, :], forward_flat)
     for copy in copies:
-        copy.wait()
+        copy.wait_recv()
     mine = jnp.sum(one_in[...], axis=0)
+    sent = copies
     copies = all_sum(mine, two_out, two_in, place_two, partner_two, 1)
+    for phase in (first, second, third):
+        phase.wait_send()
+    for copy in sent:
+        copy.wait_send()
     for copy in copies:
         copy.wait()
     cells_total = PLANES * CORE * CORE * ny * nx
@@ -510,13 +545,12 @@
             pltpu.VMEM((256, 128), BF16),
             pltpu.VMEM((256, 384), F32),
             pltpu.VMEM((3, 4, PATCH, 128), F32),
-            pltpu.VMEM((3, PATCH, 128), F32),
-            pltpu.VMEM((3, 4, 32, PATCH), F32),
-            pltpu.VMEM((2, 2, 4, 8, 128), F32),
-            pltpu.VMEM((3, 4, 32, PATCH), F32),
-            pltpu.VMEM((2, 4, 8, 128), F32),
-            pltpu.VMEM((2, 4, 16, 128), F32),
-            pltpu.VMEM((4, 16, 128), F32),
+            pltpu.VMEM((3, 2, 64, 128), BF16),
+            pltpu.VMEM((3, 2, 64, 128), BF16),
+            pltpu.VMEM((3, 32, 128), BF16),
+            pltpu.VMEM((3, 2, 64, 128), BF16),
+            pltpu.VMEM((3, 2, 64, 128), BF16),
+            pltpu.VMEM((3, 4, 16, 128), BF16),
             pltpu.VMEM((FLAT, 128), F32),
             pltpu.VMEM((FLAT, 128), F32),
             pltpu.VMEM((1, 128), F32),

time: 45.6 us -> 44.2 us (0.969)
  Pallas kernels: 44.8 us -> 43.5 us
    pallas_call x1, Pallas kernels: 44 us -> 42.7 us  [body(): pl.pallas_call(functools.partial(kernel, ny, nx), out_shape=(pltpu.VMEM((...]
where the time goes in v4:
time: 44.2 us; the launch traced here: 44.1 us
  Pallas kernels  43.5 us (98%)
  between operations  0.64 us (1%)
    pallas_call x1, Pallas kernels, body(): pl.pallas_call(functools.partial(kernel, ny, nx), out_shape=(pltpu.VMEM((...  42.7 us

profile of v4, /device:TPU:1, one launch (start us, length us, event | category | flops | bytes accessed | tf_op | source)
XLA Modules:
  0.0 44.1 jit_solution(3419694394820882659)
XLA Ops:
  0.6 42.7 %step.1 = (f32[392,128]{1,0:T(8,128)S(1)}, f32[392,128]{1,0:T(8,128)S(1)}, f32[2,2,3]{2,1,0:T(2,128)S(1)}) custom-call(f32[392,128]{1,0:T(8,128)} %bitcast.4, bf16[1,1,32,32,32]{4,3,2,1,0:T(8,128)(2,1)} %taps_hbm.1, s32[1,1,2]{2,1,0:T(1,128)} %offsets_hbm.1, s32[128,128]{1,0:T(8,128)} %mask_hbm.1, bf16[256,256]{1,0:T(8,128)(2,1)} %constant.8.clone.forward_hbm, ...), custom_call_target="tpu_custom_call" | custom-call | tf_op jit(solution)/shard_map/step/pallas_call | solution.py:532
  43.4 0.8 %store.1 = (f32[392,128]{1,0:T(8,128)}, f32[392,128]{1,0:T(8,128)}, f32[2,2,3]{2,1,0:T(2,128)}) custom-call(f32[392,128]{1,0:T(8,128)S(1)} %get-tuple-element.9.object_vmem, f32[392,128]{1,0:T(8,128)S(1)} %get-tuple-element.10.image_vmem, f32[2,2,3]{2,1,0:T(2,128)S(1)} %get-tuple-element.11.factors_vmem), custom_call_target="tpu_custom_call" | custom-call | tf_op jit(solution)/shard_map/store/pallas_call | solution.py:572

commit v5 on v4

--- a/solution.py
+++ b/solution.py
@@ -82,32 +82,27 @@
         self.there = [there for *_, there in plan]
         self.back = [self.there[i] for i in (1, 0, 3, 2, 7, 6, 5, 4)]
 
-    def pack(self, planes, starting=False):
-        def start(*which):
-            for i in which if starting else ():
-                pl.when(self.there[i])(self.copies[i].start)
-
-        lane = lax.broadcasted_iota(jnp.int32, (PATCH, 128), 1)
-        height, (top, bottom) = self.height, self.rows
-        packed = roll(planes[0], 16)
-        for m in range(1, 2 * PLANES):
-            packed = jnp.where(lane >= 32 * m, roll(planes[m], 16 + 32 * m), packed)
-        ends = jnp.concatenate([packed[top : top + height], packed[bottom : bottom + height]], axis=0)
-        self.corner_out[0 : 2 * height, :] = ends.astype(BF16)
-        start(4, 5, 6, 7)
-        turned = packed.T
+    def begin(self, *which):
+        for i in which:
+            pl.when(self.there[i])(self.copies[i].start)
+
+    def pack_columns(self, strip_of):
         for side, first in enumerate(self.cols_out):
-            strips = [turned[32 * m + first : 32 * m + first + height] for m in range(2 * PLANES)]
-            self.col_out[side, 0 : 4 * height, :] = jnp.concatenate(strips, axis=0).astype(BF16)
-        start(2, 3)
+            strips = [strip_of(m)[first : first + self.height] for m in range(2 * PLANES)]
+            self.col_out[side, 0 : 4 * self.height, :] = jnp.concatenate(strips, axis=0).astype(BF16)
+
+    def pack_rows(self, planes):
+        height = self.height
+        lane = lax.broadcasted_iota(jnp.int32, (height, 128), 1)
+        ends = []
         for side, first in enumerate(self.rows):
             strips = [planes[m][first : first + height] for m in range(2 * PLANES)]
             self.row_out[side, 0 : 4 * height, :] = jnp.concatenate(strips, axis=0).astype(BF16)
-        start(0, 1)
-
-    def start(self):
-        for i in (4, 5, 6, 7, 2, 3, 0, 1):
-            pl.when(self.there[i])(self.copies[i].start)
+            packed = roll(strips[0], 16)
+            for m in range(1, 2 * PLANES):
+                packed = jnp.where(lane >= 32 * m, roll(strips[m], 16 + 32 * m), packed)
+            ends.append(packed)
+        self.corner_out[0 : 2 * height, :] = jnp.concatenate(ends, axis=0).astype(BF16)
 
     def wait_recv(self):
         for copy, there in zip(self.copies, self.back):
@@ -156,7 +151,7 @@
     return first, second
 
 
-def blur(cells, spectrum, forward_ref, backward_ref, adjoint):
+def blur(cells, spectrum, forward_ref, backward_ref, adjoint, send_ends):
     half = PATCH
     table, turned = forward_ref[...], backward_ref[...]
     values = jnp.concatenate(
@@ -197,6 +192,12 @@
         ],
         axis=0,
     )
+    ends = [table[at : at + 16] for k in range(2) for at in (k * half + half - 16, k * half)]
+    ends = lax.dot_general(
+        jnp.concatenate(ends, axis=0), swapped, (((1,), (1,)), ((), ())), preferred_element_type=F32
+    )
+    ends = [[ends[32 * k : 32 * (k + 1), z * half : (z + 1) * half] for z in range(PLANES)] for k in range(2)]
+    send_ends(ends)
     back_x = mm(swapped, turned)
     return [[back_x[z * half : (z + 1) * half, k * half : (k + 1) * half] for z in range(PLANES)] for k in range(2)]
 
@@ -303,9 +304,15 @@
                 both = jnp.where(lane14 >= 128 - 16 * k, low_part, high_part)
             planes[0, m, pl.ds(HALF + k, 14, stride=8), :] = roll(both, 16 * k + HALF)
 
-    first.pack([planes[0, m] for m in range(4)])
+    measured_planes = [planes[0, m] for m in range(4)]
+    packed = roll(measured_planes[0], 16)
+    for m in range(1, 4):
+        packed = jnp.where(lane >= 32 * m, roll(measured_planes[m], 16 + 32 * m), packed)
+    packed = packed.T
+    first.pack_columns(lambda m: packed[32 * m : 32 * (m + 1)])
+    first.pack_rows(measured_planes)
     pl.semaphore_wait(barrier, greeted)
-    first.start()
+    first.begin(4, 5, 6, 7, 2, 3, 0, 1)
 
     for load in loads[1:5]:
         load.wait()
@@ -334,6 +341,8 @@
     for load in loads[5:]:
         load.wait()
     weight = mask[...].astype(F32)
+    weight_ends = weight.T
+    weight_ends = jnp.concatenate([weight_ends[PATCH - 16 :], weight_ends[:16]], axis=0)
 
     def tile(left, right):
         return jnp.sum((left * right).reshape(-1, 8, 128), axis=0)
@@ -360,13 +369,20 @@
         centre = jnp.concatenate([up_rows[m], planes[0, m, owned, :], down_rows[m]], axis=0)
         cells = jnp.where(owned_lane, centre, roll(columns, -16 - 32 * m))
         window[m // 2][m % 2] = jnp.where(inside, cells, 0.0)
-    result = restored(blur(normalised(window, scalars), spectrum_ref[...], forward_ref, backward_ref, True), factor)
+    def send_second(ends):
+        ends = restored(ends, factor)
+        second.pack_columns(lambda m: ends[m // 2][m % 2] * weight_ends)
+        second.begin(2, 3)
+
+    unit = normalised(window, scalars)
+    result = restored(blur(unit, spectrum_ref[...], forward_ref, backward_ref, True, send_second), factor)
     result = [result[m // 2][m % 2] * weight for m in range(4)]
-    second.pack(result, starting=True)
+    second.pack_rows(result)
+    second.begin(4, 5, 6, 7, 0, 1)
     for m in range(4):
         planes[1, m] = result[m]
     pairs = ((0, 0), (0, 1), (1, 1))
-    scalars, factor = scalars_of(grams((result[:2], result[2:]), (result[:2], result[2:]), pairs))
+    scalars, next_factor = scalars_of(grams((result[:2], result[2:]), (result[:2], result[2:]), pairs))
 
     second.wait_recv()
     columns, upper, lower = second.sides()
@@ -383,9 +399,16 @@
         cells = cells + jnp.where(edge_lane, roll(columns, -16 - 32 * m), 0.0)
         planes[1, m] = cells
         window[m // 2][m % 2] = cells * keep
-    result = restored(blur(normalised(window, scalars), spectrum_ref[...], forward_ref, backward_ref, False), factor)
+    def send_third(ends):
+        ends = restored(ends, next_factor)
+        third.pack_columns(lambda m: ends[m // 2][m % 2])
+        third.begin(2, 3)
+
+    unit = normalised(window, scalars)
+    result = restored(blur(unit, spectrum_ref[...], forward_ref, backward_ref, False, send_third), next_factor)
     result = [result[m // 2][m % 2] for m in range(4)]
-    third.pack(result, starting=True)
+    third.pack_rows(result)
+    third.begin(4, 5, 6, 7, 0, 1)
     for m in range(4):
         planes[2, m] = result[m]
     own_v = [[jnp.where(owned_core, planes[1, 2 * k + z, owned, :], 0.0) for z in range(PLANES)] for k in range(2)]

time: 44.2 us -> 44 us (level)
  no operation moved by 1% of the time
where the time goes in v5:
time: 44 us; the launch traced here: 43.9 us
  Pallas kernels  43.2 us (98%)
  between operations  0.64 us (1%)
    pallas_call x1, Pallas kernels, body(): pl.pallas_call(functools.partial(kernel, ny, nx), out_shape=(pltpu.VMEM((...  42.5 us

profile of v5, /device:TPU:1, one launch (start us, length us, event | category | flops | bytes accessed | tf_op | source)
XLA Modules:
  0.0 43.9 jit_solution(13585826410158431823)
XLA Ops:
  0.6 42.5 %step.1 = (f32[392,128]{1,0:T(8,128)S(1)}, f32[392,128]{1,0:T(8,128)S(1)}, f32[2,2,3]{2,1,0:T(2,128)S(1)}) custom-call(f32[392,128]{1,0:T(8,128)} %bitcast.4, bf16[1,1,32,32,32]{4,3,2,1,0:T(8,128)(2,1)} %taps_hbm.1, s32[1,1,2]{2,1,0:T(1,128)} %offsets_hbm.1, s32[128,128]{1,0:T(8,128)} %mask_hbm.1, bf16[256,256]{1,0:T(8,128)(2,1)} %constant.8.clone.forward_hbm, ...), custom_call_target="tpu_custom_call" | custom-call | tf_op jit(solution)/shard_map/step/pallas_call | solution.py:555
  43.1 0.8 %store.1 = (f32[392,128]{1,0:T(8,128)}, f32[392,128]{1,0:T(8,128)}, f32[2,2,3]{2,1,0:T(2,128)}) custom-call(f32[392,128]{1,0:T(8,128)S(1)} %get-tuple-element.9.object_vmem, f32[392,128]{1,0:T(8,128)S(1)} %get-tuple-element.10.image_vmem, f32[2,2,3]{2,1,0:T(2,128)S(1)} %get-tuple-element.11.factors_vmem), custom_call_target="tpu_custom_call" | custom-call | tf_op jit(solution)/shard_map/store/pallas_call | solution.py:595

commit v6 on v5

--- a/solution.py
+++ b/solution.py
@@ -209,10 +209,12 @@
 
 
 def factor_of(g00, g01, g11):
-    r00 = jnp.sqrt(jnp.maximum(g00, 0.0) + EPSILON)
-    r01 = g01 / r00
-    r11 = jnp.sqrt(jnp.maximum(g11 - r01 * r01, 0.0) + EPSILON)
-    return r00, r01, r11
+    s00 = jnp.maximum(g00, 0.0) + EPSILON
+    i00 = lax.rsqrt(s00)
+    r01 = g01 * i00
+    s11 = jnp.maximum(g11 - r01 * r01, 0.0) + EPSILON
+    i11 = lax.rsqrt(s11)
+    return (s00 * i00, r01, s11 * i11), (i00, i11)
 
 
 def kernel(
@@ -312,7 +314,7 @@
     first.pack_columns(lambda m: packed[32 * m : 32 * (m + 1)])
     first.pack_rows(measured_planes)
     pl.semaphore_wait(barrier, greeted)
-    first.begin(4, 5, 6, 7, 2, 3, 0, 1)
+    first.begin(2, 3, 4, 5, 6, 7, 0, 1)
 
     for load in loads[1:5]:
         load.wait()
@@ -486,16 +488,15 @@
     m00, m01, m11, v00, v01, v11, f00, f01, f11, p00, p01, p10, p11 = [
         jnp.sum(jnp.where(lane1 == q, gathered, 0.0), axis=1, keepdims=True) for q in range(13)
     ]
-    a, b, c = factor_of(m00, m01, m11)
-    u00, u11 = 1.0 / a, 1.0 / c
+    (a, b, c), (u00, u11) = factor_of(m00, m01, m11)
     u01 = -b * u00 * u11
     w00 = u00 * u00 * v00
     w01 = u00 * (u01 * v00 + u11 * v01)
     w11 = u01 * u01 * v00 + 2.0 * u01 * u11 * v01 + u11 * u11 * v11
-    alpha, beta, gamma = factor_of(w00, w01, w11)
-    t00 = u00 / alpha
-    t11 = u11 / gamma
-    t01 = (u01 - beta * t00) / gamma
+    (alpha, beta, gamma), (per_alpha, per_gamma) = factor_of(w00, w01, w11)
+    t00 = u00 * per_alpha
+    t11 = u11 * per_gamma
+    t01 = (u01 - beta * t00) * per_gamma
     x0, x1 = alpha * u00 + beta * u01, beta * u11
     y0, y1 = gamma * u01, gamma * u11
 
@@ -509,9 +510,11 @@
 
     zero = jnp.zeros_like(a)
     z_first, z_second = (t00, zero, x0, x1), (t01, t11, y0, y1)
-    rho, sigma, tau = factor_of(form(z_first, z_first), form(z_first, z_second), form(z_second, z_second))
-    i0 = [value / rho for value in z_first]
-    i1 = [(value - sigma * lead) / tau for value, lead in zip(z_second, i0)]
+    (rho, sigma, tau), (per_rho, per_tau) = factor_of(
+        form(z_first, z_first), form(z_first, z_second), form(z_second, z_second)
+    )
+    i0 = [value * per_rho for value in z_first]
+    i1 = [(value - sigma * lead) * per_tau for value, lead in zip(z_second, i0)]
 
     half = FLAT // 2
     one, two = slice(0, half), slice(half, FLAT)

time: 44 us -> 43.9 us (level)
  no operation moved by 1% of the time
where the time goes in v6:
time: 43.9 us; the launch traced here: 43.8 us
  Pallas kernels  43.2 us (98%)
  between operations  0.64 us (1%)
    pallas_call x1, Pallas kernels, body(): pl.pallas_call(functools.partial(kernel, ny, nx), out_shape=(pltpu.VMEM((...  42.4 us

profile of v6, /device:TPU:1, one launch (start us, length us, event | category | flops | bytes accessed | tf_op | source)
XLA Modules:
  0.0 43.8 jit_solution(11603663910532455541)
XLA Ops:
  0.6 42.4 %step.1 = (f32[392,128]{1,0:T(8,128)S(1)}, f32[392,128]{1,0:T(8,128)S(1)}, f32[2,2,3]{2,1,0:T(2,128)S(1)}) custom-call(f32[392,128]{1,0:T(8,128)} %bitcast.4, bf16[1,1,32,32,32]{4,3,2,1,0:T(8,128)(2,1)} %taps_hbm.1, s32[1,1,2]{2,1,0:T(1,128)} %offsets_hbm.1, s32[128,128]{1,0:T(8,128)} %mask_hbm.1, bf16[256,256]{1,0:T(8,128)(2,1)} %constant.8.clone.forward_hbm, ...), custom_call_target="tpu_custom_call" | custom-call | tf_op jit(solution)/shard_map/step/pallas_call | solution.py:558
  43.0 0.8 %store.1 = (f32[392,128]{1,0:T(8,128)}, f32[392,128]{1,0:T(8,128)}, f32[2,2,3]{2,1,0:T(2,128)}) custom-call(f32[392,128]{1,0:T(8,128)S(1)} %get-tuple-element.9.object_vmem, f32[392,128]{1,0:T(8,128)S(1)} %get-tuple-element.10.image_vmem, f32[2,2,3]{2,1,0:T(2,128)S(1)} %get-tuple-element.11.factors_vmem), custom_call_target="tpu_custom_call" | custom-call | tf_op jit(solution)/shard_map/store/pallas_call | solution.py:598

commit v7 on v6

--- a/solution.py
+++ b/solution.py
@@ -537,12 +537,11 @@
 
 
 def store(object_vmem, image_vmem, factors_vmem, object_hbm, image_hbm, factors_hbm, sem):
-    copies = [
-        pltpu.make_async_copy(source, target, sem.at[i])
-        for i, (source, target) in enumerate(
-            ((object_vmem, object_hbm), (image_vmem, image_hbm), (factors_vmem, factors_hbm))
-        )
-    ]
+    pairs = [(factors_vmem, factors_hbm)]
+    for first, last in ((0, 104), (104, 200), (200, 296), (296, FLAT)):
+        rows = pl.ds(first, last - first)
+        pairs += [(object_vmem.at[rows], object_hbm.at[rows]), (image_vmem.at[rows], image_hbm.at[rows])]
+    copies = [pltpu.make_async_copy(source, target, sem.at[i]) for i, (source, target) in enumerate(pairs)]
     for copy in copies:
         copy.start()
     for copy in copies:
@@ -600,7 +599,7 @@
         out_shape=(pltpu.HBM((FLAT, 128), F32), pltpu.HBM((FLAT, 128), F32), pltpu.HBM((2, 2, 3), F32)),
         in_specs=[vmem] * 3,
         out_specs=(hbm, hbm, hbm),
-        scratch_shapes=[pltpu.SemaphoreType.DMA((3,))],
+        scratch_shapes=[pltpu.SemaphoreType.DMA((9,))],
         name="store",
     )(*results)
     shape = (2, PLANES, 1, 1, CORE * CORE)

time: 43.9 us -> 44 us (level)
  no operation moved by 1% of the time
where the time goes in v7:
time: 44 us; the launch traced here: 43.9 us
  Pallas kernels  43.2 us (98%)
  between operations  0.64 us (1%)
    pallas_call x1, Pallas kernels, body(): pl.pallas_call(functools.partial(kernel, ny, nx), out_shape=(pltpu.VMEM((...  42.4 us

profile of v7, /device:TPU:1, one launch (start us, length us, event | category | flops | bytes accessed | tf_op | source)
XLA Modules:
  0.0 43.9 jit_solution(3928373391987519877)
XLA Ops:
  0.6 42.4 %step.1 = (f32[392,128]{1,0:T(8,128)S(1)}, f32[392,128]{1,0:T(8,128)S(1)}, f32[2,2,3]{2,1,0:T(2,128)S(1)}) custom-call(f32[392,128]{1,0:T(8,128)} %bitcast.4, bf16[1,1,32,32,32]{4,3,2,1,0:T(8,128)(2,1)} %taps_hbm.1, s32[1,1,2]{2,1,0:T(1,128)} %offsets_hbm.1, s32[128,128]{1,0:T(8,128)} %mask_hbm.1, bf16[256,256]{1,0:T(8,128)(2,1)} %constant.8.clone.forward_hbm, ...), custom_call_target="tpu_custom_call" | custom-call | tf_op jit(solution)/shard_map/step/pallas_call | solution.py:557
  43.0 0.8 %store.1 = (f32[392,128]{1,0:T(8,128)}, f32[392,128]{1,0:T(8,128)}, f32[2,2,3]{2,1,0:T(2,128)}) custom-call(f32[392,128]{1,0:T(8,128)S(1)} %get-tuple-element.9.object_vmem, f32[392,128]{1,0:T(8,128)S(1)} %get-tuple-element.10.image_vmem, f32[2,2,3]{2,1,0:T(2,128)S(1)} %get-tuple-element.11.factors_vmem), custom_call_target="tpu_custom_call" | custom-call | tf_op jit(solution)/shard_map/store/pallas_call | solution.py:597
